TPU v7x, 128 devices: a whole 4x4x4 slice. The times are simulated.
128 devices in a mesh: space: 16 (over y, z_hi, core), chaos: 8 (over x, z_lo).
Axes of the slice: x: 4, y: 4, z: 4 (z_hi: 2, z_lo: 2; z = z_hi * 2 + z_lo), core: 2. Of those that a mesh axis runs over, the one named last changes fastest.
Arguments:
- forcing: float32 [288, 256, 128], P('chaos', 'space'), may hold values from -12 to 12, as said below
- start_guess: float32 [288, 256, 128], P('chaos', 'space'), may hold values from -2 to 2, as said below
- mean_field: float32 [256, 128], P('space'), may hold values from 1 to 2
- mode_fields: float32 [10, 256, 128], P(None, 'space'), may hold values from -0.04 to 0.04
- multi_index: int32 [288, 10], P('chaos'), may hold values from -1 to 3, as said below
- coupled_slot: int32 [288, 20], P('chaos'), may hold values from 0 to 288, as said below
Outputs:
- approximation: float32 [288, 256, 128], P('chaos', 'space')
- recursive_residual: float32 [288, 256, 128], P('chaos', 'space')
Inputs may be any that keep to these rules, and one draw needn't show every extreme that they name: `multi_index`: row s is the multi-index of the chaos term placed in slot s: 10 nonnegative entries summing to at most 3, each such multi-index in exactly one slot; the slots without a term hold -1 in every entry. `coupled_slot`: entry (s, k) for k < 10 is the slot whose multi-index is that of slot s with one more in mode k, entry (s, 10 + k) the slot with one less in mode k; 288 where no such term exists or slot s holds no term. `forcing`: zero in the slots that hold no term. `start_guess`: zero in the slots that hold no term.
All inputs are finite; a program needn't handle non-finite values.
Results may differ from a plain program's by a relative error of at most 0.0003.
Values sent between devices are 32-bit elements; how exact they have to be, the bound alone decides.
A program may use at most 128 MiB of HBM per device.

v0:
```python
import jax
import jax.numpy as jnp
from jax import lax
from jax.sharding import PartitionSpec as P

ITERS = 2


def with_halo(value, sides, width):
    for axis, dim in sides:
        size, length = (lax.axis_size(axis), value.shape[dim])
        up = [(i, (i + 1) % size) for i in range(size - 1)]
        down = [(j, i) for i, j in up]
        last = lax.slice_in_dim(value, length - width, length, axis=dim)
        first = lax.slice_in_dim(value, 0, width, axis=dim)
        before = lax.ppermute(last, axis, up)
        after = lax.ppermute(first, axis, down)
        value = jnp.concatenate([before, value, after], axis=dim)
    return value


def stencil(values, coeffs):
    col_faces = 0.5 * (coeffs[1:] + coeffs[:-1])
    col_flux = col_faces * (values[:, 1:] - values[:, :-1])
    across = col_flux[:, :-1] - col_flux[:, 1:]
    inner_coef = jnp.pad(coeffs[1:-1], ((0, 0), (1, 1)))
    inner_vals = jnp.pad(values[:, 1:-1], ((0, 0), (0, 0), (1, 1)))
    row_faces = 0.5 * (inner_coef[:, 1:] + inner_coef[:, :-1])
    row_flux = row_faces * (inner_vals[:, :, 1:] - inner_vals[:, :, :-1])
    return across + row_flux[:, :, :-1] - row_flux[:, :, 1:]


def weights_of(multi_index, coupled_slot, slot_count):
    mode_count = multi_index.shape[1]
    degrees = multi_index.astype(jnp.float32)
    raise_weight = jnp.where(
        coupled_slot[:, :mode_count] < slot_count, jnp.sqrt(degrees + 1.0), 0.0
    )
    lower_weight = jnp.sqrt(jnp.maximum(degrees, 0.0))
    return (raise_weight, lower_weight)


def operate_gathered(term_field, coeff_ext, multi_index, coupled_slot):
    mode_count = multi_index.shape[1]
    slot_count = lax.axis_size("chaos") * term_field.shape[0]
    raise_weight, lower_weight = weights_of(multi_index, coupled_slot, slot_count)
    raise_index = jnp.minimum(coupled_slot[:, :mode_count], slot_count - 1)
    lower_index = jnp.minimum(coupled_slot[:, mode_count:], slot_count - 1)
    extended = with_halo(term_field, (("space", 1),), 1)
    result = stencil(extended, coeff_ext[0])
    everything = lax.all_gather(extended, "chaos", axis=0, tiled=True)
    for kl_mode in range(mode_count):
        mixture = raise_weight[:, kl_mode, None, None] * everything[raise_index[:, kl_mode]]
        mixture = (
            mixture + lower_weight[:, kl_mode, None, None] * everything[lower_index[:, kl_mode]]
        )
        result = result + stencil(mixture, coeff_ext[kl_mode + 1])
    return result


def squares(residual):
    return lax.psum(jnp.sum(residual * residual), ("space", "chaos"))


def curving(direction, applied):
    return lax.psum(jnp.sum(direction * applied), ("space", "chaos"))


def solve_steps(apply_op, forcing, start_guess):
    approximation = start_guess
    residual = forcing - apply_op(start_guess)
    direction = residual
    norm_now = squares(residual)
    for number in range(ITERS):
        applied = apply_op(direction)
        step_length = norm_now / curving(direction, applied)
        approximation = approximation + step_length * direction
        residual = residual - step_length * applied
        if number + 1 < ITERS:
            norm_next = squares(residual)
            direction = residual + norm_next / norm_now * direction
            norm_now = norm_next
    return (approximation, residual)


def per_device(forcing, start_guess, mean_field, mode_fields, multi_index, coupled_slot):
    stacked = jnp.concatenate([mean_field[None], mode_fields], axis=0)
    coeff_ext = with_halo(stacked, (("space", 1),), 1)

    def apply_op(term_field):
        return operate_gathered(term_field, coeff_ext, multi_index, coupled_slot)

    return solve_steps(apply_op, forcing, start_guess)


def solution(mesh):
    placed = (
        P("chaos", "space", None),
        P("chaos", "space", None),
        P("space", None),
        P(None, "space", None),
        P("chaos", None),
        P("chaos", None),
    )
    return jax.shard_map(
        per_device,
        mesh=mesh,
        in_specs=placed,
        out_specs=(P("chaos", "space", None), P("chaos", "space", None)),
        check_vma=False,
    )
```

profile of v0, /device:TPU:0, one launch (start us, length us, event | category | flops | bytes accessed | tf_op | source)
XLA Modules:
  0.0 738.5 jit_solution(6637280891308617727)
XLA Ops:
  17.4 6.2 collective-permute-start.1
  42.8 57.3 %all-gather.4.cloned.1.call-done = f32[288,18,128]{2,1,0:T(8,128)} async-done(((f32[36,18,128]{2,1,0:T(8,128)}), f32[288,18,128]{2,1,0:T(8,128)}) %all-gather.4.cloned.1.call-update) | async-done | bytes 2654224 | tf_op jit(solution)/shard_map/all_gather | solution.py:51
  100.1 3.6 gather_fusion.19
  103.7 3.5 gather_fusion.18
  181.5 81.4 %all-gather.6.cloned.1.call-done = f32[288,18,128]{2,1,0:T(8,128)} async-done(((f32[36,18,128]{2,1,0:T(8,128)}), f32[288,18,128]{2,1,0:T(8,128)}) %all-gather.6.cloned.1.call-update) | async-done | bytes 2654224 | tf_op jit(solution)/shard_map/all_gather | solution.py:51
  291.2 3.5 gather_fusion.30
  297.4 3.5 gather_fusion.29
  300.9 3.5 gather_fusion.28
  308.0 3.5 gather_fusion.27
  311.5 3.5 gather_fusion.26
  318.5 3.5 gather_fusion.25
  332.5 3.5 gather_fusion.22
  339.5 3.5 gather_fusion.21
  343.0 3.5 gather_fusion.20
  354.3 66.2 %all-reduce.44 = (f32[]{:T(128)}, f32[]{:T(128)}) all-reduce(f32[]{:T(128)} %get-tuple-element.3, f32[]{:T(128)} %get-tuple-element.2), channel_id=1, replica_groups=mesh['space'=16,'chaos'=8] {'space','chaos'}, use_global_device_ids=true, to_apply=%region_1.2 | all-reduce | flops 2 | bytes 16 | tf_op jit(solution)/shard_map/psum | solution.py:62
  422.5 62.3 %psum.30 = f32[]{:T(128)} all-reduce(f32[]{:T(128)} %multiply_reduce_fusion.1), channel_id=1, replica_groups=mesh['space'=16,'chaos'=8] {'space','chaos'}, use_global_device_ids=true, to_apply=%region_5.6 | all-reduce | flops 1 | bytes 8 | tf_op jit(solution)/shard_map/psum | solution.py:62
  493.4 79.3 %all-gather.8.cloned.1.call-done = f32[288,18,128]{2,1,0:T(8,128)} async-done(((f32[36,18,128]{2,1,0:T(8,128)}), f32[288,18,128]{2,1,0:T(8,128)}) %all-gather.8.cloned.1.call-update) | async-done | bytes 2654224 | tf_op jit(solution)/shard_map/all_gather | solution.py:51
  602.4 3.5 gather_fusion.50
  612.0 3.5 gather_fusion.48
  621.7 3.5 gather_fusion.46
  631.3 3.5 gather_fusion.44
  640.9 3.5 gather_fusion.42
  650.6 3.5 gather_fusion.40
  662.6 66.1 %psum.31 = f32[]{:T(128)} all-reduce(f32[]{:T(128)} %get-tuple-element.6), channel_id=1, replica_groups=mesh['space'=16,'chaos'=8] {'space','chaos'}, use_global_device_ids=true, to_apply=%region_7.8 | all-reduce | flops 1 | bytes 8 | tf_op jit(solution)/shard_map/psum | solution.py:66
  (423 shorter events, 240.5 us)
Async XLA Ops:
  7.2 92.9 %all-gather.4.cloned.1.call-start = ((), (), s32[]{:S(2)}) async-start(), calls=%async_computation | async-start | bytes 3981312 | tf_op jit(solution)/shard_map/all_gather | solution.py:51
  8.3 4.3 collective-permute-start.2
  9.6 3.9 collective-permute-start.3
  15.3 247.7 %all-gather.6.cloned.1.call-start = ((), (), s32[]{:S(2)}) async-start(), calls=%async_computation.1 | async-start | bytes 3981312 | tf_op jit(solution)/shard_map/all_gather | solution.py:51
  16.1 23.5 %collective-permute-start = (f32[11,1,128]{2,1,0:T(1,128)S(1)}, f32[11,1,128]{2,1,0:T(1,128)S(1)}, u32[]{:S(2)}, u32[]{:S(2)}) collective-permute-start(f32[11,1,128]{2,1,0:T(1,128)S(1)} %get-tuple-element.30), channel_id=1, source_target_pairs={{8,0},{16,8},{24,16},{32,24},{40,32},{48,40},{56,48},{64,56},{72,6... | collective-permute-start | bytes 16904 | tf_op jit(solution)/shard_map/ppermute | solution.py:17
  17.4 22.2 %collective-permute-start.1 = (f32[11,1,128]{2,1,0:T(1,128)S(1)}, f32[11,1,128]{2,1,0:T(1,128)S(1)}, u32[]{:S(2)}, u32[]{:S(2)}) collective-permute-start(f32[11,1,128]{2,1,0:T(1,128)S(1)} %get-tuple-element.31), channel_id=1, source_target_pairs={{0,8},{8,16},{16,24},{24,32},{32,40},{40,48},{48,56},{56,64},{64,7... | collective-permute-start | bytes 16904 | tf_op jit(solution)/shard_map/ppermute | solution.py:16
  174.0 94.3 %copy-start.91 = (f32[36]{0:T(128)S(1)}, f32[36]{0:T(128)}, u32[]{:S(2)}) copy-start(f32[36]{0:T(128)} %get-tuple-element.55) | copy-start | bytes 436
  174.0 94.3 %copy-start.95 = (f32[36]{0:T(128)S(1)}, f32[36]{0:T(128)}, u32[]{:S(2)}) copy-start(f32[36]{0:T(128)} %get-tuple-element.45) | copy-start | bytes 436
  174.0 94.5 %copy-start.80 = (f32[17,128]{1,0:T(8,128)S(1)}, f32[17,128]{1,0:T(8,128)}, u32[]{:S(2)}) copy-start(f32[17,128]{1,0:T(8,128)} %get-tuple-element.18) | copy-start | bytes 26116
  174.1 4.3 collective-permute-start.4
  175.4 3.9 collective-permute-start.5
  180.1 392.6 %all-gather.8.cloned.1.call-start = ((), (), s32[]{:S(2)}) async-start(), calls=%async_computation.2 | async-start | bytes 3981312 | tf_op jit(solution)/shard_map/all_gather | solution.py:51
  181.5 92.6 %copy-start.87 = (f32[36]{0:T(128)S(1)}, f32[36]{0:T(128)}, u32[]{:S(2)}) copy-start(f32[36]{0:T(128)} %get-tuple-element.56) | copy-start | bytes 436
  181.5 92.6 %copy-start.93 = (f32[36]{0:T(128)S(1)}, f32[36]{0:T(128)}, u32[]{:S(2)}) copy-start(f32[36]{0:T(128)} %get-tuple-element.46) | copy-start | bytes 436
  352.2 140.1 %copy-start.75 = (f32[16,129]{1,0:T(8,128)S(1)}, f32[16,129]{1,0:T(8,128)}, u32[]{:S(2)}) copy-start(f32[16,129]{1,0:T(8,128)} %copy-done.73) | copy-start | bytes 24772
  354.2 139.0 %copy-start.84 = (f32[17,128]{1,0:T(8,128)S(1)}, f32[17,128]{1,0:T(8,128)}, u32[]{:S(2)}) copy-start(f32[17,128]{1,0:T(8,128)} %copy-done.82) | copy-start | bytes 26116
  354.3 223.8 %copy-start.92 = (f32[36]{0:T(128)S(1)}, f32[36]{0:T(128)}, u32[]{:S(2)}) copy-start(f32[36]{0:T(128)} %get-tuple-element.55) | copy-start | bytes 436
  354.3 223.9 %copy-start.96 = (f32[36]{0:T(128)S(1)}, f32[36]{0:T(128)}, u32[]{:S(2)}) copy-start(f32[36]{0:T(128)} %get-tuple-element.45) | copy-start | bytes 436
  486.1 92.9 %copy-start.81 = (f32[17,128]{1,0:T(8,128)S(1)}, f32[17,128]{1,0:T(8,128)}, u32[]{:S(2)}) copy-start(f32[17,128]{1,0:T(8,128)} %get-tuple-element.18) | copy-start | bytes 26116
  486.2 4.6 collective-permute-start.6
  487.5 3.9 collective-permute-start.7
  493.4 91.2 %copy-start.88 = (f32[36]{0:T(128)S(1)}, f32[36]{0:T(128)}, u32[]{:S(2)}) copy-start(f32[36]{0:T(128)} %get-tuple-element.56) | copy-start | bytes 436
  493.4 91.2 %copy-start.94 = (f32[36]{0:T(128)S(1)}, f32[36]{0:T(128)}, u32[]{:S(2)}) copy-start(f32[36]{0:T(128)} %get-tuple-element.46) | copy-start | bytes 436
  660.0 70.1 %copy-start.2 = (f32[36,16,128]{2,1,0:T(8,128)S(1)}, f32[36,16,128]{2,1,0:T(8,128)}, u32[]{:S(2)}) copy-start(f32[36,16,128]{2,1,0:T(8,128)} %param.7) | copy-start | bytes 884740
  (84 other events, 360.8 us)
Sparse Core Ops, SparseCore 0:
  15.4 84.6 all-gather.3
  180.2 82.6 all-gather.5
  492.3 80.2 all-gather.7
where the time goes:
time: 744 us; the launch traced here: 738 us
  waiting for transfers between devices  220 us (30%)
  blocking collectives  195 us (26%)
  local copies, waits for them, and re-layouts  178 us (24%)
  other arithmetic  105 us (14%)
  starting transfers between devices  20.9 us (3%)
  between operations  19.8 us (3%)
    all_gather x3, waiting for transfers between devices, operate_gathered(): everything = lax.all_gather(extended, 'chaos', axis=0, tiled=True)  218 us
    psum x2, blocking collectives, squares(): return lax.psum(jnp.sum(residual * residual), ('space', 'chaos'))  128 us
    gather x30, local copies, waits for them, and re-layouts, operate_gathered(): everything[raise_index[:, kl_mode]]  80.2 us
    gather x30, local copies, waits for them, and re-layouts, operate_gathered(): everything[lower_index[:, kl_mode]]  74.8 us
    psum x1, blocking collectives, curving(): return lax.psum(jnp.sum(direction * applied), ('space', 'chaos'))  66.1 us
    mul x35, other arithmetic, stencil(): col_flux = col_faces * (values[:, 1:] - values[:, :-1])  35.2 us
    add x30, other arithmetic, operate_gathered(): mixture + lower_weight[:, kl_mode, None, None] * everything[lower_index[:...  30.2 us
    slice x30, local copies, waits for them, and re-layouts, stencil(): inner_vals = jnp.pad(values[:, 1:-1], ((0, 0), (0, 0), (1, 1)))  18.9 us
  transfers between devices with their start and end apart: 11, of which 6 were waited for; matrix products, arithmetic and copies ran while one was open for 3% of the time, Pallas kernels for 0%

commit v1 on v0

v1 whole, which is shorter than its diff:
```python
import functools
import math

import jax
import jax.numpy as jnp
import numpy as np
from jax import lax
from jax.experimental import pallas as pl
from jax.experimental.pallas import tpu as pltpu
from jax.sharding import PartitionSpec as P

MESH = pl.DeviceIdType.MESH
F32 = jnp.float32
DEGREE = 3
LANES = 128
PAD = 40


def term_list(modes, degree):
    def build(count, left):
        if count == 0:
            return [()]
        return [(a,) + tail for a in range(left + 1) for tail in build(count - 1, left - a)]

    return sorted(build(modes, degree), key=sum)


def code_of(term):
    return sum(m * 4**k for k, m in enumerate(term))


def kernel(
    cfg,
    f_ref,
    x_ref,
    mean_ref,
    modes_ref,
    index_ref,
    code_ref,
    xo_ref,
    ro_ref,
    sbx,
    sbf,
    scode,
    scoef,
    rx,
    rf,
    rcode,
    rcoef,
    pick,
    field,
    forced,
    halo,
    grad,
    flux,
    faces,
    outs,
    back,
    dot_local,
    dot_a,
    dot_b_local,
    dot_b,
    sx,
    sf,
    sc,
    sk,
    sh,
    so,
    sda,
    sdb,
    qx,
    qf,
    qc,
    qk,
    qh,
    qo,
    qda,
    qdb,
):
    slots, cols, terms, modes = cfg["slots"], cfg["cols"], cfg["terms"], cfg["modes"]
    rows = cfg["rows"]
    full = cfg["full"]
    position = {t: i for i, t in enumerate(terms)}

    space, chaos = lax.axis_index("space"), lax.axis_index("chaos")
    pair, core = space // 2, space % 2
    xx, zz = chaos // 2, chaos % 2
    lane_at = xx + zz * (3 - 2 * xx)
    member = 8 * zz + 2 * lane_at + core
    me = 16 * pair + member
    last = 127

    def device(j):
        p = (j // 2) % 8
        z = p // 4
        inner = p % 4
        x = inner + z * (3 - 2 * inner)
        return (2 * (j // 16) + j % 2, 2 * x + z)

    def remote(src, dst, ssem, rsem, where):
        return pltpu.make_async_remote_copy(
            src_ref=src, dst_ref=dst, send_sem=ssem, recv_sem=rsem, device_id=where, device_id_type=MESH
        )

    barrier = pltpu.get_barrier_semaphore()

    def greet(j):
        pl.semaphore_signal(barrier, inc=1, device_id=device(j), device_id_type=MESH)

    for o in range(1, 16):
        greet(16 * pair + (member + o) % 16)
    for o in range(1, 8):
        greet(16 * ((pair + o) % 8) + member)
    pl.when(me > 0)(lambda: greet(me - 1))
    pl.when(me < last)(lambda: greet(me + 1))

    zero8 = jnp.zeros((8, LANES), F32)
    for c in range(cols):
        for src, dst in ((x_ref, sbx), (f_ref, sbf)):
            dst[c, 32:40, :] = zero8
            dst[c, 0:slots, :] = src[pl.ds(c, slots, stride=cols), :]
    power = jnp.left_shift(1, 2 * lax.broadcasted_iota(jnp.int32, (1, modes), 1)).astype(F32)
    code = jnp.sum(index_ref[...].astype(F32) * power, axis=1, keepdims=True)
    at_sub = lax.broadcasted_iota(jnp.int32, (slots, LANES), 0)
    at_lane = lax.broadcasted_iota(jnp.int32, (slots, LANES), 1)
    row = jnp.sum(jnp.where(at_sub == at_lane, code, 0.0), axis=0, keepdims=True)
    lane1 = lax.broadcasted_iota(jnp.int32, (1, LANES), 1)
    row = jnp.where(lane1 < slots, row, -1.0)
    scode[...] = jnp.broadcast_to(row, (8, LANES))

    mine = 2 * lane_at + core
    other = 2 * lane_at + (1 - core)
    for which, first in ((0, 2 * mine), (1, 2 * other)):
        for c in range(2):
            scoef[which, c, 8:16, :] = zero8
            scoef[which, c, 0:1, :] = mean_ref[pl.ds(first + c, 1), :]
            for k in range(modes):
                scoef[which, c, 1 + k : 2 + k, :] = modes_ref[k, pl.ds(first + c, 1), :]

    @pl.when(me == 0)
    def _():
        for i in range(3):
            halo[i, 0] = jnp.zeros((full, LANES), F32)

    @pl.when(me == last)
    def _():
        for i in range(3):
            halo[i, 1] = jnp.zeros((full, LANES), F32)

    greeted = 15 + 7 + jnp.where(me > 0, 1, 0) + jnp.where(me < last, 1, 0)
    pl.semaphore_wait(barrier, greeted)

    def piece(send, land, ssem, rsem, i):
        where = device(8 * space + i)
        return remote(send, land, ssem.at[i], rsem.at[chaos], where)

    def scatter(copy_of, keep):
        for o in range(8):
            i = (o + chaos) % 8
            target = 8 * space + i
            pl.when(target != me)(lambda: copy_of(i).start())
            pl.when(target == me)(lambda: keep(i))

    own_source = (me // 8) == space

    def arrive(copy_of):
        for g in range(8):
            here = jnp.logical_and(own_source, chaos == g)
            pl.when(jnp.logical_not(here))(lambda: copy_of(g).wait_recv())

    def code_copy(i):
        return piece(scode, rcode.at[chaos], sc, qc, i)

    def x_copy(i):
        return piece(sbx.at[pl.ds(2 * i, 2)], rx.at[chaos], sx, qx, i)

    def f_copy(i):
        return piece(sbf.at[pl.ds(2 * i, 2)], rf.at[chaos], sf, qf, i)

    def keep_code(i):
        rcode[chaos] = scode[...]

    def keep_x(i):
        rx[chaos] = sbx[pl.ds(2 * i, 2)]

    def keep_f(i):
        rf[chaos] = sbf[pl.ds(2 * i, 2)]

    sibling = me + 1 - 2 * core
    coef_copy = remote(scoef.at[1], rcoef, sk, qk, device(sibling))
    scatter(code_copy, keep_code)
    coef_copy.start()
    scatter(x_copy, keep_x)
    scatter(f_copy, keep_f)

    def code_wait(g):
        return remote(scode, rcode.at[g], sc.at[0], qc.at[g], device(me))

    def x_wait(g):
        return remote(sbx.at[0:2], rx.at[g], sx.at[0], qx.at[g], device(me))

    def f_wait(g):
        return remote(sbf.at[0:2], rf.at[g], sf.at[0], qf.at[g], device(me))

    arrive(code_wait)
    sub40 = lax.broadcasted_iota(jnp.int32, (PAD, LANES), 0)
    lane40 = lax.broadcasted_iota(jnp.int32, (PAD, LANES), 1)
    for g in range(8):
        spread = jnp.where(sub40 == lane40, rcode[g, 0:1, :], 0.0)
        placed = jnp.sum(spread, axis=1, keepdims=True)
        pick[PAD * g : PAD * (g + 1), :] = jnp.where(placed == code_ref[0:1, :], 1.0, 0.0)

    def parts(value):
        high = value.astype(jnp.bfloat16)
        rest = value - high.astype(F32)
        mid = rest.astype(jnp.bfloat16)
        low = (rest - mid.astype(F32)).astype(jnp.bfloat16)
        return [high, mid, low]

    def select(first, second, transposed):
        both = parts(first) + parts(second)
        return lax.dot_general(
            pick[...].astype(jnp.bfloat16),
            jnp.concatenate(both, axis=1),
            (((0 if transposed else 1,), (0,)), ((), ())),
            preferred_element_type=F32,
        )

    def column(result, c):
        base = 3 * LANES * c
        return (
            result[:, base : base + LANES]
            + result[:, base + LANES : base + 2 * LANES]
            + result[:, base + 2 * LANES : base + 3 * LANES]
        )

    coef_copy.wait_recv()
    local = core == zz
    for c in range(2):
        field[0, c, rows:full, :] = jnp.where(local, scoef[0, c], rcoef[c])

    arrive(x_wait)
    got = select(rx[:, 0].reshape(8 * PAD, LANES), rx[:, 1].reshape(8 * PAD, LANES), True)
    for c in range(2):
        field[0, c, 0:rows, :] = column(got, c)[0:rows]

    def halo_left(i):
        return remote(field.at[i, 0], halo.at[i, 1], sh.at[i, 0], qh.at[i, 1], device(me - 1))

    def halo_right(i):
        return remote(field.at[i, 1], halo.at[i, 0], sh.at[i, 1], qh.at[i, 0], device(me + 1))

    def halo_start(i):
        pl.when(me > 0)(lambda: halo_left(i).start())
        pl.when(me < last)(lambda: halo_right(i).start())

    def halo_wait(i):
        pl.when(me > 0)(lambda: halo_right(i).wait_recv())
        pl.when(me < last)(lambda: halo_left(i).wait_recv())

    halo_start(0)

    arrive(f_wait)
    got = select(rf[:, 0].reshape(8 * PAD, LANES), rf[:, 1].reshape(8 * PAD, LANES), True)
    for c in range(2):
        forced[c] = column(got, c)[0:rows]

    lane8 = lax.broadcasted_iota(jnp.int32, (8, LANES), 1)

    def back_copy(i, g):
        return remote(
            outs.at[i, g],
            back.at[i, pl.ds(2 * (me % 8), 2)],
            so.at[i, g],
            qo.at[i, me % 8],
            (me // 8, g),
        )

    def back_wait(i, j):
        return remote(outs.at[i, 0], back.at[i, pl.ds(2 * j, 2)], so.at[i, 0], qo.at[i, j], (space, chaos))

    def send_back(i):
        got = select(field[i + 1, 0, 0:rows, :], field[i + 1, 1, 0:rows, :], False)
        for c in range(2):
            whole = column(got, c)
            for g in range(8):
                outs[i, g, c] = whole[PAD * g : PAD * (g + 1)]
        for o in range(8):
            g = (o + chaos) % 8
            here = jnp.logical_and(own_source, g == chaos)
            pl.when(jnp.logical_not(here))(lambda: back_copy(i, g).start())

            @pl.when(here)
            def _():
                back[i, pl.ds(2 * (me % 8), 2)] = outs[i, g]

    def dots(which, values):
        dot_local[which] = zero8
        for n, value in enumerate(values):
            dot_local[which, n : n + 1, :] = jnp.sum(value, axis=0, keepdims=True)

    def dot_a_copy(which, o):
        return remote(
            dot_local.at[which],
            dot_a.at[which, member],
            sda.at[which, o],
            qda.at[which, member],
            device(16 * pair + (member + o) % 16),
        )

    def dot_b_copy(which, o):
        return remote(
            dot_b_local.at[which],
            dot_b.at[which, pair],
            sdb.at[which, o],
            qdb.at[which, pair],
            device(16 * ((pair + o) % 8) + member),
        )

    def dot_a_start(which):
        for o in range(1, 16):
            dot_a_copy(which, o).start()
        dot_a[which, member] = dot_local[which]

    def dot_b_start(which):
        for o in range(1, 16):
            m = (member + o) % 16
            remote(
                dot_local.at[which], dot_a.at[which, m], sda.at[which, 0], qda.at[which, m], device(me)
            ).wait_recv()
        total = dot_a[which, 0]
        for m in range(1, 16):
            total = total + dot_a[which, m]
        dot_b_local[which] = total
        for o in range(1, 8):
            dot_b_copy(which, o).start()
        dot_b[which, pair] = total

    def dot_total(which):
        for o in range(1, 8):
            m = (pair + o) % 8
            remote(
                dot_b_local.at[which], dot_b.at[which, m], sdb.at[which, 0], qdb.at[which, m], device(me)
            ).wait_recv()
        total = dot_b[which, 0]
        for m in range(1, 8):
            total = total + dot_b[which, m]
        return jnp.sum(total, axis=1, keepdims=True)

    def chunk_sum(first, second):
        return jnp.sum((first * second).reshape(-1, 8, LANES), axis=0)

    def apply(i, carry):
        halo_wait(i)

        @pl.when(i == 0)
        def _():
            for h in range(2):
                part = pl.ds(rows + 8 * h, 8)
                left, c0, c1, right = halo[0, 0, part], field[0, 0, part], field[0, 1, part], halo[0, 1, part]

                def up(value):
                    return jnp.where(lane8 < LANES - 1, pltpu.roll(value, LANES - 1, 1), 0.0)

                kinds = [
                    0.5 * (left + c0),
                    0.5 * (c0 + c1),
                    0.5 * (c1 + right),
                    0.5 * (c0 + up(c0)),
                    0.5 * (c1 + up(c1)),
                    jnp.where(lane8 == 0, 0.5 * c0, 0.0),
                    jnp.where(lane8 == 0, 0.5 * c1, 0.0),
                    zero8,
                ]
                for n, kind in enumerate(kinds):
                    faces[pl.ds(64 * h + n, 8, stride=8), :] = kind

        def gradients(b, carry):
            part = pl.ds(pl.multiple_of(8 * b, 8), 8)
            left, u0, u1, right = halo[i, 0, part], field[i, 0, part], field[i, 1, part], halo[i, 1, part]
            up0 = jnp.where(lane8 < LANES - 1, pltpu.roll(u0, LANES - 1, 1), 0.0)
            up1 = jnp.where(lane8 < LANES - 1, pltpu.roll(u1, LANES - 1, 1), 0.0)
            kinds = [u0 - left, u1 - u0, right - u1, up0 - u0, up1 - u1]
            kinds += [jnp.where(lane8 == 0, u0, 0.0), jnp.where(lane8 == 0, u1, 0.0), zero8]
            for n, kind in enumerate(kinds):
                grad[pl.ds(64 * b + n, 8, stride=8), :] = kind
            return carry

        lax.fori_loop(0, rows // 8, gradients, 0, unroll=4)

        weight = [faces[8 * k : 8 * (k + 1), :] for k in range(modes + 1)]
        for s, term in enumerate(terms):
            total = weight[0] * grad[8 * s : 8 * (s + 1), :]
            for k in range(modes):
                mix = None
                for step, square in ((1, term[k] + 1), (-1, term[k])):
                    near = term[:k] + (term[k] + step,) + term[k + 1 :]
                    if near not in position:
                        continue
                    at = position[near]
                    value = grad[8 * at : 8 * (at + 1), :]
                    if square > 1:
                        value = math.sqrt(square) * value
                    mix = value if mix is None else mix + value
                if mix is not None:
                    total = total + weight[k + 1] * mix
            flux[8 * s : 8 * (s + 1), :] = total
        for s in range(len(terms), rows):
            flux[8 * s : 8 * (s + 1), :] = zero8

        def divergence(b, carry):
            kind = [flux[pl.ds(64 * b + n, 8, stride=8), :] for n in range(7)]
            part = pl.ds(pl.multiple_of(8 * b, 8), 8)
            for c in range(2):
                down = jnp.where(lane8 > 0, pltpu.roll(kind[3 + c], 1, 1), kind[5 + c])
                value = kind[c] - kind[c + 1] + down - kind[3 + c]
                field[i + 1, c, part, :] = jnp.where(i == 0, forced[c, part, :] - value, value)
            return carry

        lax.fori_loop(0, rows // 8, divergence, 0, unroll=4)
        pl.when(i < 2)(lambda: halo_start(i + 1))
        send_back(i)

        @pl.when(i == 1)
        def _():
            r, w = field[1, :, 0:rows, :], field[2, :, 0:rows, :]
            dots(0, [chunk_sum(r, r), chunk_sum(r, w)])
            dot_a_start(0)

        return carry

    lax.fori_loop(0, 3, apply, 0)

    dot_b_start(0)
    sums = dot_total(0)
    rr, rw = sums[0:1], sums[1:2]
    alpha = rr / rw
    r0, w, v = field[1, :, 0:rows, :], field[2, :, 0:rows, :], field[3, :, 0:rows, :]
    r1 = r0 - alpha * w
    ar1 = w - alpha * v
    dots(1, [chunk_sum(r1, r1), chunk_sum(r1, ar1), chunk_sum(r1, w) + chunk_sum(r0, ar1)])
    dot_a_start(1)
    dot_b_start(1)
    sums = dot_total(1)
    rr1 = sums[0:1]
    beta = rr1 / rr
    step = rr1 / (sums[1:2] + beta * sums[2:3] + beta * beta * rw)

    for j in range(8):
        here = jnp.logical_and(own_source, me % 8 == j)
        for i in range(3):
            pl.when(jnp.logical_not(here))(lambda: back_wait(i, j).wait_recv())

    for c in range(cols):
        r0, w, v = back[0, c, 0:slots], back[1, c, 0:slots], back[2, c, 0:slots]
        x = x_ref[pl.ds(c, slots, stride=cols), :]
        xo_ref[pl.ds(c, slots, stride=cols), :] = x + (alpha + step + step * beta) * r0 - (step * alpha) * w
        r1 = r0 - alpha * w
        ro_ref[pl.ds(c, slots, stride=cols), :] = r1 - step * (w - alpha * v + beta * w)

    for i in range(8):
        target = 8 * space + i

        @pl.when(target != me)
        def _():
            code_copy(i).wait_send()
            x_copy(i).wait_send()
            f_copy(i).wait_send()

    coef_copy.wait_send()
    for i in range(3):
        pl.when(me > 0)(lambda: halo_left(i).wait_send())
        pl.when(me < last)(lambda: halo_right(i).wait_send())
        for g in range(8):
            here = jnp.logical_and(own_source, chaos == g)
            pl.when(jnp.logical_not(here))(lambda: back_copy(i, g).wait_send())
    for which in range(2):
        for o in range(1, 16):
            dot_a_copy(which, o).wait_send()
        for o in range(1, 8):
            dot_b_copy(which, o).wait_send()


def per_device(forcing, start_guess, mean_field, mode_fields, multi_index, coupled_slot):
    slots, cols, lanes = forcing.shape
    modes = mode_fields.shape[0]
    terms = term_list(modes, DEGREE)
    rows = -(-len(terms) // 8) * 8
    full = rows + 16
    wide = rows
    codes = np.full((8, wide), -2.0, np.float32)
    codes[:, : len(terms)] = [code_of(t) for t in terms]
    cfg = dict(slots=slots, cols=cols, terms=terms, modes=modes, rows=rows, full=full)
    flat = jax.ShapeDtypeStruct((slots * cols, lanes), F32)
    vmem = pl.BlockSpec(memory_space=pltpu.VMEM)
    dma, V = pltpu.SemaphoreType.DMA, pltpu.VMEM
    scratch = [
        V((cols, PAD, lanes), F32),
        V((cols, PAD, lanes), F32),
        V((8, lanes), F32),
        V((2, 2, 16, lanes), F32),
        V((8, 2, PAD, lanes), F32),
        V((8, 2, PAD, lanes), F32),
        V((8, 8, lanes), F32),
        V((2, 16, lanes), F32),
        V((8 * PAD, wide), F32),
        V((4, 2, full, lanes), F32),
        V((2, rows, lanes), F32),
        V((3, 2, full, lanes), F32),
        V((8 * rows, lanes), F32),
        V((8 * rows, lanes), F32),
        V((128, lanes), F32),
        V((3, 8, 2, PAD, lanes), F32),
        V((3, cols, PAD, lanes), F32),
        V((2, 8, lanes), F32),
        V((2, 16, 8, lanes), F32),
        V((2, 8, lanes), F32),
        V((2, 8, 8, lanes), F32),
        dma((8,)),
        dma((8,)),
        dma((8,)),
        dma,
        dma((3, 2)),
        dma((3, 8)),
        dma((2, 16)),
        dma((2, 8)),
        dma((8,)),
        dma((8,)),
        dma((8,)),
        dma,
        dma((3, 2)),
        dma((3, 8)),
        dma((2, 16)),
        dma((2, 8)),
    ]
    x, r = pl.pallas_call(
        functools.partial(kernel, cfg),
        out_shape=(flat, flat),
        in_specs=[vmem] * 6,
        out_specs=(vmem, vmem),
        scratch_shapes=scratch,
        compiler_params=pltpu.CompilerParams(
            collective_id=0, has_side_effects=True, vmem_limit_bytes=48 * 2**20
        ),
    )(
        forcing.reshape(slots * cols, lanes),
        start_guess.reshape(slots * cols, lanes),
        mean_field,
        mode_fields,
        multi_index,
        jnp.asarray(codes),
    )
    return (x.reshape(slots, cols, lanes), r.reshape(slots, cols, lanes))


def solution(mesh):
    placed = (
        P("chaos", "space", None),
        P("chaos", "space", None),
        P("space", None),
        P(None, "space", None),
        P("chaos", None),
        P("chaos", None),
    )
    return jax.shard_map(
        per_device,
        mesh=mesh,
        in_specs=placed,
        out_specs=(P("chaos", "space", None), P("chaos", "space", None)),
        check_vma=False,
    )
```

time: 744 us -> 61 us (0.08)
  waiting for transfers between devices: 220 us -> 0 us
  blocking collectives: 195 us -> 0 us
  local copies, waits for them, and re-layouts: 178 us -> 5.04 us
  other arithmetic: 105 us -> 0 us
  Pallas kernels: 0 us -> 54.6 us
  starting transfers between devices: 20.9 us -> 0 us
  between operations: 19.8 us -> 0.67 us
    all_gather x3 -> x0, waiting for transfers between devices: 218 us -> none  [operate_gathered(): everything = lax.all_gather(extended, 'chaos', axis=0, tiled=True)]
    psum x3 -> x0, blocking collectives: 195 us -> none  [the longest x2 128 us: squares(): return lax.psum(jnp.sum(residual * residual), ('space', 'chaos'))]
    gather x60 -> x0, local copies, waits for them, and re-layouts: 155 us -> none  [the longest x30 80.2 us: operate_gathered(): everything[raise_index[:, kl_mode]]]
    pallas_call x0 -> x1, Pallas kernels: none -> 54.6 us  [per_device(): pl.pallas_call(functools.partial(kernel, cfg), out_shape=(flat, flat), in...]
    mul x74 -> x0, other arithmetic: 53.2 us -> none  [the longest x35 35.2 us: stencil(): col_flux = col_faces * (values[:, 1:] - values[:, :-1])]
    add x31 -> x0, other arithmetic: 30.3 us -> none  [the longest x30 30.2 us: operate_gathered(): mixture + lower_weight[:, kl_mode, None, None] * everything[lower_index[:...]
    slice x34 -> x0, local copies, waits for them, and re-layouts: 20.9 us -> none  [the longest x30 18.9 us: stencil(): inner_vals = jnp.pad(values[:, 1:-1], ((0, 0), (0, 0), (1, 1)))]
    ppermute x8 -> x0, starting transfers between devices: 20.6 us -> none  [the longest x4 15.5 us: with_halo(): before = lax.ppermute(last, axis, up)]
  transfers between devices with their start and end apart: 11 -> 0, of which waited for: 6 -> 0; matrix products, arithmetic and copies ran while one was open for 3% -> 0% of each run, Pallas kernels for 0% -> 0%
where the time goes in v1:
time: 61 us; the launch traced here: 60.3 us
  Pallas kernels  54.6 us (90%)
  local copies, waits for them, and re-layouts  5.04 us (8%)
  between operations  0.67 us (1%)
    pallas_call x1, Pallas kernels, per_device(): pl.pallas_call(functools.partial(kernel, cfg), out_shape=(flat, flat), in...  54.6 us
    unnamed x13, local copies, waits for them, and re-layouts  5.04 us

profile of v1, /device:TPU:0, one launch (start us, length us, event | category | flops | bytes accessed | tf_op | source)
XLA Modules:
  0.0 60.3 jit_solution(11278251941811657138)
XLA Ops:
  0.6 0.0 copy-start.3
  0.6 0.0 copy-start.4
  0.7 0.8 %copy.8.index_ref = s32[36,10]{1,0:T(8,128)S(1)} copy(s32[36,10]{0,1:T(8,128)} %param.11) | data formatting | bytes 2880 | tf_op args[4]
  1.5 0.0 copy-done.3
  1.5 0.0 copy-done.4
  1.5 0.0 copy-start
  1.5 1.0 %copy-done = f32[36,16,128]{2,1,0:T(8,128)S(1)} copy-done((f32[36,16,128]{2,1,0:T(8,128)S(1)}, f32[36,16,128]{2,1,0:T(8,128)}, u32[]{:S(2)}) %copy-start) | copy-done | bytes 294936
  2.4 0.0 copy-start.1
  2.4 1.0 %copy-done.1 = f32[36,16,128]{2,1,0:T(8,128)S(1)} copy-done((f32[36,16,128]{2,1,0:T(8,128)S(1)}, f32[36,16,128]{2,1,0:T(8,128)}, u32[]{:S(2)}) %copy-start.1) | copy-done | bytes 294936
  3.4 0.0 copy-start.2
  3.4 0.9 %copy-done.2 = f32[10,16,128]{2,1,0:T(8,128)S(1)} copy-done((f32[10,16,128]{2,1,0:T(8,128)S(1)}, f32[10,16,128]{2,1,0:T(8,128)}, u32[]{:S(2)}) %copy-start.2) | copy-done | bytes 81944
  4.3 54.6 %shard_map.77 = (f32[576,128]{1,0:T(8,128)S(1)}, f32[576,128]{1,0:T(8,128)S(1)}) custom-call(f32[576,128]{1,0:T(8,128)S(1)} %bitcast.6, f32[576,128]{1,0:T(8,128)S(1)} %bitcast.7, f32[16,128]{1,0:T(8,128)S(1)} %copy-done.4, f32[10,16,128]{2,1,0:T(8,128)S(1)} %copy-done.2, s32[36,10]{1,0:T(8,128)S(1)} %copy.8.index_ref, f32[8,288]{1,0:T(8,128)S(1)} %copy-done.3), custom_call_target="tpu_custom_call" | custom-call | tf_op jit(solution)/shard_map/pallas_call | solution.py:536
  58.9 0.7 %copy.11 = f32[36,16,128]{2,1,0:T(8,128)} copy(f32[36,16,128]{2,1,0:T(8,128)S(1)} %bitcast.5) | data formatting | bytes 589824
  59.6 0.7 %copy.12 = f32[36,16,128]{2,1,0:T(8,128)} copy(f32[36,16,128]{2,1,0:T(8,128)S(1)} %bitcast.4) | data formatting | bytes 589824
Async XLA Ops:
  0.6 0.8 %copy-start.3 = (f32[8,288]{1,0:T(8,128)S(1)}, f32[8,288]{1,0:T(8,128)}, u32[]{:S(2)}) copy-start(f32[8,288]{1,0:T(8,128)} %constant.2.clone.code_ref) | copy-start | bytes 27652
  0.6 0.8 %copy-start.4 = (f32[16,128]{1,0:T(8,128)S(1)}, f32[16,128]{1,0:T(8,128)}, u32[]{:S(2)}) copy-start(f32[16,128]{1,0:T(8,128)} %mean_ref.1) | copy-start | bytes 24580
  1.5 1.0 %copy-start = (f32[36,16,128]{2,1,0:T(8,128)S(1)}, f32[36,16,128]{2,1,0:T(8,128)}, u32[]{:S(2)}) copy-start(f32[36,16,128]{2,1,0:T(8,128)} %param.7) | copy-start | bytes 884740
  2.4 1.0 %copy-start.1 = (f32[36,16,128]{2,1,0:T(8,128)S(1)}, f32[36,16,128]{2,1,0:T(8,128)}, u32[]{:S(2)}) copy-start(f32[36,16,128]{2,1,0:T(8,128)} %param.8) | copy-start | bytes 884740
  3.4 0.9 %copy-start.2 = (f32[10,16,128]{2,1,0:T(8,128)S(1)}, f32[10,16,128]{2,1,0:T(8,128)}, u32[]{:S(2)}) copy-start(f32[10,16,128]{2,1,0:T(8,128)} %modes_ref.1) | copy-start | bytes 245764

commit v2 on v1

--- a/solution.py
+++ b/solution.py
@@ -31,14 +31,21 @@
 
 def kernel(
     cfg,
+    f_hbm,
+    x_hbm,
+    mean_hbm,
+    modes_hbm,
+    index_hbm,
+    code_hbm,
+    xo_ref,
+    ro_ref,
     f_ref,
     x_ref,
     mean_ref,
     modes_ref,
     index_ref,
     code_ref,
-    xo_ref,
-    ro_ref,
+    si,
     sbx,
     sbf,
     scode,
@@ -102,32 +109,58 @@
             src_ref=src, dst_ref=dst, send_sem=ssem, recv_sem=rsem, device_id=where, device_id_type=MESH
         )
 
+    loads = [
+        pltpu.make_async_copy(src, dst, si.at[n])
+        for n, (src, dst) in enumerate(
+            (
+                (index_hbm, index_ref),
+                (x_hbm, x_ref),
+                (mean_hbm, mean_ref),
+                (modes_hbm, modes_ref),
+                (code_hbm, code_ref),
+                (f_hbm, f_ref),
+            )
+        )
+    ]
+    for load in loads:
+        load.start()
+
+    zero8 = jnp.zeros((8, LANES), F32)
+    for g in range(8):
+        for c in range(2):
+            rx[g, c, 32:40, :] = zero8
+            rf[g, c, 32:40, :] = zero8
+
+    @pl.when(me == 0)
+    def _():
+        for i in range(3):
+            halo[i, 0] = jnp.zeros((full, LANES), F32)
+
+    @pl.when(me == last)
+    def _():
+        for i in range(3):
+            halo[i, 1] = jnp.zeros((full, LANES), F32)
+
     barrier = pltpu.get_barrier_semaphore()
 
     def greet(j):
         pl.semaphore_signal(barrier, inc=1, device_id=device(j), device_id_type=MESH)
 
+    for o in range(1, 8):
+        greet(16 * ((pair + o) % 8) + member)
     for o in range(1, 16):
         greet(16 * pair + (member + o) % 16)
-    for o in range(1, 8):
-        greet(16 * ((pair + o) % 8) + member)
     pl.when(me > 0)(lambda: greet(me - 1))
     pl.when(me < last)(lambda: greet(me + 1))
 
-    zero8 = jnp.zeros((8, LANES), F32)
-    for c in range(cols):
-        for src, dst in ((x_ref, sbx), (f_ref, sbf)):
-            dst[c, 32:40, :] = zero8
-            dst[c, 0:slots, :] = src[pl.ds(c, slots, stride=cols), :]
-    power = jnp.left_shift(1, 2 * lax.broadcasted_iota(jnp.int32, (1, modes), 1)).astype(F32)
-    code = jnp.sum(index_ref[...].astype(F32) * power, axis=1, keepdims=True)
-    at_sub = lax.broadcasted_iota(jnp.int32, (slots, LANES), 0)
-    at_lane = lax.broadcasted_iota(jnp.int32, (slots, LANES), 1)
-    row = jnp.sum(jnp.where(at_sub == at_lane, code, 0.0), axis=0, keepdims=True)
-    lane1 = lax.broadcasted_iota(jnp.int32, (1, LANES), 1)
-    row = jnp.where(lane1 < slots, row, -1.0)
-    scode[...] = jnp.broadcast_to(row, (8, LANES))
-
+    loads[0].wait()
+    power = jnp.left_shift(1, 2 * lax.broadcasted_iota(jnp.int32, (modes, slots), 0)).astype(F32)
+    code = jnp.sum(index_ref[...].astype(F32) * power, axis=0, keepdims=True)
+    scode[...] = jnp.full((8, LANES), -1.0, F32)
+    scode[:, 0:slots] = jnp.broadcast_to(code, (8, slots))
+
+    loads[2].wait()
+    loads[3].wait()
     mine = 2 * lane_at + core
     other = 2 * lane_at + (1 - core)
     for which, first in ((0, 2 * mine), (1, 2 * other)):
@@ -137,16 +170,7 @@
             for k in range(modes):
                 scoef[which, c, 1 + k : 2 + k, :] = modes_ref[k, pl.ds(first + c, 1), :]
 
-    @pl.when(me == 0)
-    def _():
-        for i in range(3):
-            halo[i, 0] = jnp.zeros((full, LANES), F32)
-
-    @pl.when(me == last)
-    def _():
-        for i in range(3):
-            halo[i, 1] = jnp.zeros((full, LANES), F32)
-
+    loads[1].wait()
     greeted = 15 + 7 + jnp.where(me > 0, 1, 0) + jnp.where(me < last, 1, 0)
     pl.semaphore_wait(barrier, greeted)
 
@@ -154,12 +178,19 @@
         where = device(8 * space + i)
         return remote(send, land, ssem.at[i], rsem.at[chaos], where)
 
-    def scatter(copy_of, keep):
+    def scatter(copy_of, keep, ready=None):
         for o in range(8):
             i = (o + chaos) % 8
             target = 8 * space + i
+            if ready is not None:
+                ready(i)
             pl.when(target != me)(lambda: copy_of(i).start())
             pl.when(target == me)(lambda: keep(i))
+
+    def sent(copy_of):
+        for i in range(8):
+            target = 8 * space + i
+            pl.when(target != me)(lambda: copy_of(i).wait_send())
 
     own_source = (me // 8) == space
 
@@ -172,37 +203,53 @@
         return piece(scode, rcode.at[chaos], sc, qc, i)
 
     def x_copy(i):
-        return piece(sbx.at[pl.ds(2 * i, 2)], rx.at[chaos], sx, qx, i)
+        return piece(
+            sbx.at[pl.ds(2 * i, 2), pl.ds(0, slots)], rx.at[chaos, :, pl.ds(0, slots)], sx, qx, i
+        )
 
     def f_copy(i):
-        return piece(sbf.at[pl.ds(2 * i, 2)], rf.at[chaos], sf, qf, i)
+        return piece(
+            sbf.at[pl.ds(2 * i, 2), pl.ds(0, slots)], rf.at[chaos, :, pl.ds(0, slots)], sf, qf, i
+        )
 
     def keep_code(i):
         rcode[chaos] = scode[...]
 
-    def keep_x(i):
-        rx[chaos] = sbx[pl.ds(2 * i, 2)]
-
-    def keep_f(i):
-        rf[chaos] = sbf[pl.ds(2 * i, 2)]
+    def keep(land, send):
+        def run(i):
+            for c in range(2):
+                land[chaos, c, 0:slots, :] = send[2 * i + c, 0:slots, :]
+
+        return run
+
+    def packed(src, dst):
+        def run(i):
+            for c in range(2):
+                dst[2 * i + c, 0:slots, :] = src[pl.ds(2 * i + c, slots, stride=cols), :]
+
+        return run
 
     sibling = me + 1 - 2 * core
     coef_copy = remote(scoef.at[1], rcoef, sk, qk, device(sibling))
     scatter(code_copy, keep_code)
     coef_copy.start()
-    scatter(x_copy, keep_x)
-    scatter(f_copy, keep_f)
+    scatter(x_copy, keep(rx, sbx), packed(x_ref, sbx))
 
     def code_wait(g):
         return remote(scode, rcode.at[g], sc.at[0], qc.at[g], device(me))
 
     def x_wait(g):
-        return remote(sbx.at[0:2], rx.at[g], sx.at[0], qx.at[g], device(me))
+        return remote(
+            sbx.at[0:2, pl.ds(0, slots)], rx.at[g, :, pl.ds(0, slots)], sx.at[0], qx.at[g], device(me)
+        )
 
     def f_wait(g):
-        return remote(sbf.at[0:2], rf.at[g], sf.at[0], qf.at[g], device(me))
+        return remote(
+            sbf.at[0:2, pl.ds(0, slots)], rf.at[g, :, pl.ds(0, slots)], sf.at[0], qf.at[g], device(me)
+        )
 
     arrive(code_wait)
+    loads[4].wait()
     sub40 = lax.broadcasted_iota(jnp.int32, (PAD, LANES), 0)
     lane40 = lax.broadcasted_iota(jnp.int32, (PAD, LANES), 1)
     for g in range(8):
@@ -234,6 +281,10 @@
             + result[:, base + 2 * LANES : base + 3 * LANES]
         )
 
+    loads[5].wait()
+    sent(x_copy)
+    scatter(f_copy, keep(rf, sbf), packed(f_ref, sbf))
+
     coef_copy.wait_recv()
     local = core == zz
     for c in range(2):
@@ -244,47 +295,66 @@
     for c in range(2):
         field[0, c, 0:rows, :] = column(got, c)[0:rows]
 
-    def halo_left(i):
-        return remote(field.at[i, 0], halo.at[i, 1], sh.at[i, 0], qh.at[i, 1], device(me - 1))
-
-    def halo_right(i):
-        return remote(field.at[i, 1], halo.at[i, 0], sh.at[i, 1], qh.at[i, 0], device(me + 1))
-
-    def halo_start(i):
-        pl.when(me > 0)(lambda: halo_left(i).start())
-        pl.when(me < last)(lambda: halo_right(i).start())
-
-    def halo_wait(i):
-        pl.when(me > 0)(lambda: halo_right(i).wait_recv())
-        pl.when(me < last)(lambda: halo_left(i).wait_recv())
-
-    halo_start(0)
-
-    arrive(f_wait)
-    got = select(rf[:, 0].reshape(8 * PAD, LANES), rf[:, 1].reshape(8 * PAD, LANES), True)
-    for c in range(2):
-        forced[c] = column(got, c)[0:rows]
+    def halo_left(i, count):
+        return remote(
+            field.at[i, 0, pl.ds(0, count)],
+            halo.at[i, 1, pl.ds(0, count)],
+            sh.at[i, 0],
+            qh.at[i, 1],
+            device(me - 1),
+        )
+
+    def halo_right(i, count):
+        return remote(
+            field.at[i, 1, pl.ds(0, count)],
+            halo.at[i, 0, pl.ds(0, count)],
+            sh.at[i, 1],
+            qh.at[i, 0],
+            device(me + 1),
+        )
+
+    def halo_start(i, count):
+        pl.when(me > 0)(lambda: halo_left(i, count).start())
+        pl.when(me < last)(lambda: halo_right(i, count).start())
+
+    def halo_wait(i, count):
+        pl.when(me > 0)(lambda: halo_right(i, count).wait_recv())
+        pl.when(me < last)(lambda: halo_left(i, count).wait_recv())
+
+    def halo_sent(i, count):
+        pl.when(me > 0)(lambda: halo_left(i, count).wait_send())
+        pl.when(me < last)(lambda: halo_right(i, count).wait_send())
+
+    halo_start(0, full)
 
     lane8 = lax.broadcasted_iota(jnp.int32, (8, LANES), 1)
 
     def back_copy(i, g):
         return remote(
-            outs.at[i, g],
-            back.at[i, pl.ds(2 * (me % 8), 2)],
+            outs.at[i, g, :, pl.ds(0, slots)],
+            back.at[i, pl.ds(2 * (me % 8), 2), pl.ds(0, slots)],
             so.at[i, g],
             qo.at[i, me % 8],
             (me // 8, g),
         )
 
     def back_wait(i, j):
-        return remote(outs.at[i, 0], back.at[i, pl.ds(2 * j, 2)], so.at[i, 0], qo.at[i, j], (space, chaos))
-
-    def send_back(i):
+        return remote(
+            outs.at[i, 0, :, pl.ds(0, slots)],
+            back.at[i, pl.ds(2 * j, 2), pl.ds(0, slots)],
+            so.at[i, 0],
+            qo.at[i, j],
+            (space, chaos),
+        )
+
+    def prepare_back(i):
         got = select(field[i + 1, 0, 0:rows, :], field[i + 1, 1, 0:rows, :], False)
         for c in range(2):
             whole = column(got, c)
             for g in range(8):
                 outs[i, g, c] = whole[PAD * g : PAD * (g + 1)]
+
+    def send_back(i):
         for o in range(8):
             g = (o + chaos) % 8
             here = jnp.logical_and(own_source, g == chaos)
@@ -292,7 +362,7 @@
 
             @pl.when(here)
             def _():
-                back[i, pl.ds(2 * (me % 8), 2)] = outs[i, g]
+                back[i, pl.ds(2 * (me % 8), 2), 0:slots] = outs[i, g, :, 0:slots]
 
     def dots(which, values):
         dot_local[which] = zero8
@@ -347,36 +417,33 @@
             total = total + dot_b[which, m]
         return jnp.sum(total, axis=1, keepdims=True)
 
-    def chunk_sum(first, second):
-        return jnp.sum((first * second).reshape(-1, 8, LANES), axis=0)
-
-    def apply(i, carry):
-        halo_wait(i)
-
-        @pl.when(i == 0)
-        def _():
-            for h in range(2):
-                part = pl.ds(rows + 8 * h, 8)
-                left, c0, c1, right = halo[0, 0, part], field[0, 0, part], field[0, 1, part], halo[0, 1, part]
-
-                def up(value):
-                    return jnp.where(lane8 < LANES - 1, pltpu.roll(value, LANES - 1, 1), 0.0)
-
-                kinds = [
-                    0.5 * (left + c0),
-                    0.5 * (c0 + c1),
-                    0.5 * (c1 + right),
-                    0.5 * (c0 + up(c0)),
-                    0.5 * (c1 + up(c1)),
-                    jnp.where(lane8 == 0, 0.5 * c0, 0.0),
-                    jnp.where(lane8 == 0, 0.5 * c1, 0.0),
-                    zero8,
-                ]
-                for n, kind in enumerate(kinds):
-                    faces[pl.ds(64 * h + n, 8, stride=8), :] = kind
-
-        def gradients(b, carry):
-            part = pl.ds(pl.multiple_of(8 * b, 8), 8)
+    halo_wait(0, full)
+    for h in range(2):
+        part = pl.ds(rows + 8 * h, 8)
+        left, c0, c1, right = halo[0, 0, part], field[0, 0, part], field[0, 1, part], halo[0, 1, part]
+
+        def up(value):
+            return jnp.where(lane8 < LANES - 1, pltpu.roll(value, LANES - 1, 1), 0.0)
+
+        kinds = [
+            0.5 * (left + c0),
+            0.5 * (c0 + c1),
+            0.5 * (c1 + right),
+            0.5 * (c0 + up(c0)),
+            0.5 * (c1 + up(c1)),
+            jnp.where(lane8 == 0, 0.5 * c0, 0.0),
+            jnp.where(lane8 == 0, 0.5 * c1, 0.0),
+            zero8,
+        ]
+        for n, kind in enumerate(kinds):
+            faces[pl.ds(64 * h + n, 8, stride=8), :] = kind
+
+    def total_of(sums):
+        return [sums[n : n + 1] for n in range(3)]
+
+    def gradients(i):
+        for b in range(rows // 8):
+            part = pl.ds(8 * b, 8)
             left, u0, u1, right = halo[i, 0, part], field[i, 0, part], field[i, 1, part], halo[i, 1, part]
             up0 = jnp.where(lane8 < LANES - 1, pltpu.roll(u0, LANES - 1, 1), 0.0)
             up1 = jnp.where(lane8 < LANES - 1, pltpu.roll(u1, LANES - 1, 1), 0.0)
@@ -384,10 +451,8 @@
             kinds += [jnp.where(lane8 == 0, u0, 0.0), jnp.where(lane8 == 0, u1, 0.0), zero8]
             for n, kind in enumerate(kinds):
                 grad[pl.ds(64 * b + n, 8, stride=8), :] = kind
-            return carry
-
-        lax.fori_loop(0, rows // 8, gradients, 0, unroll=4)
-
+
+    def mixing():
         weight = [faces[8 * k : 8 * (k + 1), :] for k in range(modes + 1)]
         for s, term in enumerate(terms):
             total = weight[0] * grad[8 * s : 8 * (s + 1), :]
@@ -408,43 +473,73 @@
         for s in range(len(terms), rows):
             flux[8 * s : 8 * (s + 1), :] = zero8
 
-        def divergence(b, carry):
+    def divergence(i, after):
+        for b in range(rows // 8):
             kind = [flux[pl.ds(64 * b + n, 8, stride=8), :] for n in range(7)]
-            part = pl.ds(pl.multiple_of(8 * b, 8), 8)
+            part = pl.ds(8 * b, 8)
             for c in range(2):
                 down = jnp.where(lane8 > 0, pltpu.roll(kind[3 + c], 1, 1), kind[5 + c])
-                value = kind[c] - kind[c + 1] + down - kind[3 + c]
-                field[i + 1, c, part, :] = jnp.where(i == 0, forced[c, part, :] - value, value)
-            return carry
-
-        lax.fori_loop(0, rows // 8, divergence, 0, unroll=4)
-        pl.when(i < 2)(lambda: halo_start(i + 1))
-        send_back(i)
-
-        @pl.when(i == 1)
-        def _():
-            r, w = field[1, :, 0:rows, :], field[2, :, 0:rows, :]
-            dots(0, [chunk_sum(r, r), chunk_sum(r, w)])
-            dot_a_start(0)
-
-        return carry
-
-    lax.fori_loop(0, 3, apply, 0)
-
+                after(c, part, kind[c] - kind[c + 1] + down - kind[3 + c])
+
+    gradients(0)
+    mixing()
+    arrive(f_wait)
+    got = select(rf[:, 0].reshape(8 * PAD, LANES), rf[:, 1].reshape(8 * PAD, LANES), True)
+    for c in range(2):
+        forced[c] = column(got, c)[0:rows]
+
+    def first(c, part, value):
+        field[1, c, part, :] = forced[c, part, :] - value
+
+    divergence(0, first)
+    halo_start(1, rows)
+    prepare_back(0)
+    halo_wait(1, rows)
+    send_back(0)
+
+    gradients(1)
+    mixing()
+    sums = [zero8, zero8]
+
+    def second(c, part, value):
+        field[2, c, part, :] = value
+        r = field[1, c, part, :]
+        sums[0] = sums[0] + r * r
+        sums[1] = sums[1] + r * value
+
+    divergence(1, second)
+    halo_start(2, rows)
+    dots(0, sums)
+    dot_a_start(0)
+    prepare_back(1)
+    halo_wait(2, rows)
     dot_b_start(0)
-    sums = dot_total(0)
-    rr, rw = sums[0:1], sums[1:2]
+    send_back(1)
+
+    gradients(2)
+    mixing()
+    rr, rw = total_of(dot_total(0))[0:2]
     alpha = rr / rw
-    r0, w, v = field[1, :, 0:rows, :], field[2, :, 0:rows, :], field[3, :, 0:rows, :]
-    r1 = r0 - alpha * w
-    ar1 = w - alpha * v
-    dots(1, [chunk_sum(r1, r1), chunk_sum(r1, ar1), chunk_sum(r1, w) + chunk_sum(r0, ar1)])
+    sums = [zero8, zero8, zero8]
+
+    def third(c, part, value):
+        field[3, c, part, :] = value
+        r, w = field[1, c, part, :], field[2, c, part, :]
+        r1 = r - alpha * w
+        ar1 = w - alpha * value
+        sums[0] = sums[0] + r1 * r1
+        sums[1] = sums[1] + r1 * ar1
+        sums[2] = sums[2] + (r1 * w + r * ar1)
+
+    divergence(2, third)
+    dots(1, sums)
     dot_a_start(1)
+    prepare_back(2)
+    send_back(2)
     dot_b_start(1)
-    sums = dot_total(1)
-    rr1 = sums[0:1]
+    rr1, rar, cross = total_of(dot_total(1))
     beta = rr1 / rr
-    step = rr1 / (sums[1:2] + beta * sums[2:3] + beta * beta * rw)
+    step = rr1 / (rar + beta * cross + beta * beta * rw)
 
     for j in range(8):
         here = jnp.logical_and(own_source, me % 8 == j)
@@ -458,19 +553,11 @@
         r1 = r0 - alpha * w
         ro_ref[pl.ds(c, slots, stride=cols), :] = r1 - step * (w - alpha * v + beta * w)
 
-    for i in range(8):
-        target = 8 * space + i
-
-        @pl.when(target != me)
-        def _():
-            code_copy(i).wait_send()
-            x_copy(i).wait_send()
-            f_copy(i).wait_send()
-
+    sent(code_copy)
+    sent(f_copy)
     coef_copy.wait_send()
     for i in range(3):
-        pl.when(me > 0)(lambda: halo_left(i).wait_send())
-        pl.when(me < last)(lambda: halo_right(i).wait_send())
+        halo_sent(i, rows if i else full)
         for g in range(8):
             here = jnp.logical_and(own_source, chaos == g)
             pl.when(jnp.logical_not(here))(lambda: back_copy(i, g).wait_send())
@@ -493,8 +580,16 @@
     cfg = dict(slots=slots, cols=cols, terms=terms, modes=modes, rows=rows, full=full)
     flat = jax.ShapeDtypeStruct((slots * cols, lanes), F32)
     vmem = pl.BlockSpec(memory_space=pltpu.VMEM)
+    hbm = pl.BlockSpec(memory_space=pltpu.HBM)
     dma, V = pltpu.SemaphoreType.DMA, pltpu.VMEM
     scratch = [
+        V((slots * cols, lanes), F32),
+        V((slots * cols, lanes), F32),
+        V((cols, lanes), F32),
+        V((modes, cols, lanes), F32),
+        V((modes, slots), jnp.int32),
+        V((8, wide), F32),
+        dma((6,)),
         V((cols, PAD, lanes), F32),
         V((cols, PAD, lanes), F32),
         V((8, lanes), F32),
@@ -536,18 +631,18 @@
     x, r = pl.pallas_call(
         functools.partial(kernel, cfg),
         out_shape=(flat, flat),
-        in_specs=[vmem] * 6,
+        in_specs=[hbm] * 6,
         out_specs=(vmem, vmem),
         scratch_shapes=scratch,
         compiler_params=pltpu.CompilerParams(
-            collective_id=0, has_side_effects=True, vmem_limit_bytes=48 * 2**20
+            collective_id=0, has_side_effects=True, vmem_limit_bytes=64 * 2**20
         ),
     )(
         forcing.reshape(slots * cols, lanes),
         start_guess.reshape(slots * cols, lanes),
         mean_field,
         mode_fields,
-        multi_index,
+        multi_index.T,
         jnp.asarray(codes),
     )
     return (x.reshape(slots, cols, lanes), r.reshape(slots, cols, lanes))

time: 61 us -> 54.2 us (0.89)
  Pallas kernels: 54.6 us -> 50.8 us
  local copies, waits for them, and re-layouts: 5.04 us -> 2.46 us
    pallas_call x1, Pallas kernels: 54.6 us -> 50.8 us  [per_device(): pl.pallas_call(functools.partial(kernel, cfg), out_shape=(flat, flat), in...]
    unnamed x13 -> x4, local copies, waits for them, and re-layouts: 5.04 us -> 2.46 us
where the time goes in v2:
time: 54.2 us; the launch traced here: 53.9 us
  Pallas kernels  50.8 us (94%)
  local copies, waits for them, and re-layouts  2.46 us (5%)
  between operations  0.65 us (1%)
    pallas_call x1, Pallas kernels, per_device(): pl.pallas_call(functools.partial(kernel, cfg), out_shape=(flat, flat), in...  50.8 us
    unnamed x4, local copies, waits for them, and re-layouts  2.46 us

profile of v2, /device:TPU:0, one launch (start us, length us, event | category | flops | bytes accessed | tf_op | source)
XLA Modules:
  0.0 53.9 jit_solution(7726414292210871958)
XLA Ops:
  0.6 50.8 %shard_map.77 = (f32[576,128]{1,0:T(8,128)}, f32[576,128]{1,0:T(8,128)}) custom-call(f32[576,128]{1,0:T(8,128)} %bitcast.7, f32[576,128]{1,0:T(8,128)} %bitcast.8, f32[16,128]{1,0:T(8,128)} %mean_hbm.1, f32[10,16,128]{2,1,0:T(8,128)} %modes_hbm.1, s32[10,36]{1,0:T(8,128)} %bitcast.9, f32[8,288]{1,0:T(8,128)} %constant.2.clone.code_hbm), custom_call_target="tpu_custom_call" | custom-call | tf_op jit(solution)/shard_map/pallas_call | solution.py:631
  51.4 0.0 copy-start
  51.4 1.7 %copy.10 = f32[36,16,128]{2,1,0:T(8,128)} copy(f32[36,16,128]{2,1,0:T(8,128)} %bitcast.6) | data formatting | bytes 589824
  53.2 0.0 copy-done
  53.2 0.7 %copy.11 = f32[36,16,128]{2,1,0:T(8,128)} copy(f32[36,16,128]{2,1,0:T(8,128)S(1)} %bitcast.5) | data formatting | bytes 589824
Async XLA Ops:
  51.4 1.8 %copy-start = (f32[576,128]{1,0:T(8,128)S(1)}, f32[576,128]{1,0:T(8,128)}, u32[]{:S(2)}) copy-start(f32[576,128]{1,0:T(8,128)} %get-tuple-element.5) | copy-start | bytes 884740

commit v3 on v2

--- a/solution.py
+++ b/solution.py
@@ -14,6 +14,7 @@
 DEGREE = 3
 LANES = 128
 PAD = 40
+CUTS = 4
 
 
 def term_list(modes, degree):
@@ -104,6 +105,16 @@
         x = inner + z * (3 - 2 * inner)
         return (2 * (j // 16) + j % 2, 2 * x + z)
 
+    yy, high = pair // 2, pair % 2
+    column_rank = 4 * high + 2 * zz + core
+    plane_rank = 4 * yy + xx
+
+    def in_column(r):
+        return (4 * yy + 2 * (r // 4) + r % 2, 2 * xx + (r // 2) % 2)
+
+    def in_plane(r):
+        return (4 * (r // 4) + 2 * high + core, 2 * (r % 4) + zz)
+
     def remote(src, dst, ssem, rsem, where):
         return pltpu.make_async_remote_copy(
             src_ref=src, dst_ref=dst, send_sem=ssem, recv_sem=rsem, device_id=where, device_id_type=MESH
@@ -143,15 +154,18 @@
 
     barrier = pltpu.get_barrier_semaphore()
 
-    def greet(j):
-        pl.semaphore_signal(barrier, inc=1, device_id=device(j), device_id_type=MESH)
-
+    def greet(where):
+        pl.semaphore_signal(barrier, inc=1, device_id=where, device_id_type=MESH)
+
+    for o in range(1, 16):
+        greet(in_plane((plane_rank + o) % 16))
     for o in range(1, 8):
-        greet(16 * ((pair + o) % 8) + member)
-    for o in range(1, 16):
-        greet(16 * pair + (member + o) % 16)
-    pl.when(me > 0)(lambda: greet(me - 1))
-    pl.when(me < last)(lambda: greet(me + 1))
+        greet(in_column((column_rank + o) % 8))
+    for dx in range(1, 4):
+        for other_z, other_core in ((0, 1), (1, 0), (1, 1)):
+            greet((2 * pair + (core + other_core) % 2, 2 * ((xx + dx) % 4) + (zz + other_z) % 2))
+    pl.when(me > 0)(lambda: greet(device(me - 1)))
+    pl.when(me < last)(lambda: greet(device(me + 1)))
 
     loads[0].wait()
     power = jnp.left_shift(1, 2 * lax.broadcasted_iota(jnp.int32, (modes, slots), 0)).astype(F32)
@@ -171,16 +185,20 @@
                 scoef[which, c, 1 + k : 2 + k, :] = modes_ref[k, pl.ds(first + c, 1), :]
 
     loads[1].wait()
-    greeted = 15 + 7 + jnp.where(me > 0, 1, 0) + jnp.where(me < last, 1, 0)
+    greeted = 15 + 7 + 9 + jnp.where(me > 0, 1, 0) + jnp.where(me < last, 1, 0)
     pl.semaphore_wait(barrier, greeted)
 
     def piece(send, land, ssem, rsem, i):
         where = device(8 * space + i)
         return remote(send, land, ssem.at[i], rsem.at[chaos], where)
 
+    def far_first(o):
+        target_x = (xx + (2, 2, 1, 1, 3, 3, 0, 0)[o]) % 4
+        return 2 * (target_x + core * (3 - 2 * target_x)) + o % 2
+
     def scatter(copy_of, keep, ready=None):
         for o in range(8):
-            i = (o + chaos) % 8
+            i = far_first(o)
             target = 8 * space + i
             if ready is not None:
                 ready(i)
@@ -234,6 +252,8 @@
     scatter(code_copy, keep_code)
     coef_copy.start()
     scatter(x_copy, keep(rx, sbx), packed(x_ref, sbx))
+    loads[5].wait()
+    scatter(f_copy, keep(rf, sbf), packed(f_ref, sbf))
 
     def code_wait(g):
         return remote(scode, rcode.at[g], sc.at[0], qc.at[g], device(me))
@@ -281,51 +301,46 @@
             + result[:, base + 2 * LANES : base + 3 * LANES]
         )
 
-    loads[5].wait()
-    sent(x_copy)
-    scatter(f_copy, keep(rf, sbf), packed(f_ref, sbf))
+    per = rows // CUTS
+
+    def cut(k):
+        return pl.ds(per * k, per) if k < CUTS else pl.ds(rows, full - rows)
+
+    def halo_left(i, k):
+        return remote(
+            field.at[i, 0, cut(k)], halo.at[i, 1, cut(k)], sh.at[i, k, 0], qh.at[i, k, 1], device(me - 1)
+        )
+
+    def halo_right(i, k):
+        return remote(
+            field.at[i, 1, cut(k)], halo.at[i, 0, cut(k)], sh.at[i, k, 1], qh.at[i, k, 0], device(me + 1)
+        )
+
+    def halo_start(i, k):
+        pl.when(me > 0)(lambda: halo_left(i, k).start())
+        pl.when(me < last)(lambda: halo_right(i, k).start())
+
+    def halo_wait(i, k):
+        pl.when(me > 0)(lambda: halo_right(i, k).wait_recv())
+        pl.when(me < last)(lambda: halo_left(i, k).wait_recv())
+
+    def halo_sent(i, k):
+        pl.when(me > 0)(lambda: halo_left(i, k).wait_send())
+        pl.when(me < last)(lambda: halo_right(i, k).wait_send())
 
     coef_copy.wait_recv()
     local = core == zz
     for c in range(2):
         field[0, c, rows:full, :] = jnp.where(local, scoef[0, c], rcoef[c])
+    halo_start(0, CUTS)
 
     arrive(x_wait)
     got = select(rx[:, 0].reshape(8 * PAD, LANES), rx[:, 1].reshape(8 * PAD, LANES), True)
     for c in range(2):
         field[0, c, 0:rows, :] = column(got, c)[0:rows]
 
-    def halo_left(i, count):
-        return remote(
-            field.at[i, 0, pl.ds(0, count)],
-            halo.at[i, 1, pl.ds(0, count)],
-            sh.at[i, 0],
-            qh.at[i, 1],
-            device(me - 1),
-        )
-
-    def halo_right(i, count):
-        return remote(
-            field.at[i, 1, pl.ds(0, count)],
-            halo.at[i, 0, pl.ds(0, count)],
-            sh.at[i, 1],
-            qh.at[i, 0],
-            device(me + 1),
-        )
-
-    def halo_start(i, count):
-        pl.when(me > 0)(lambda: halo_left(i, count).start())
-        pl.when(me < last)(lambda: halo_right(i, count).start())
-
-    def halo_wait(i, count):
-        pl.when(me > 0)(lambda: halo_right(i, count).wait_recv())
-        pl.when(me < last)(lambda: halo_left(i, count).wait_recv())
-
-    def halo_sent(i, count):
-        pl.when(me > 0)(lambda: halo_left(i, count).wait_send())
-        pl.when(me < last)(lambda: halo_right(i, count).wait_send())
-
-    halo_start(0, full)
+    for k in range(CUTS):
+        halo_start(0, k)
 
     lane8 = lax.broadcasted_iota(jnp.int32, (8, LANES), 1)
 
@@ -372,52 +387,52 @@
     def dot_a_copy(which, o):
         return remote(
             dot_local.at[which],
-            dot_a.at[which, member],
+            dot_a.at[which, column_rank],
             sda.at[which, o],
-            qda.at[which, member],
-            device(16 * pair + (member + o) % 16),
+            qda.at[which, column_rank],
+            in_column((column_rank + o) % 8),
         )
 
     def dot_b_copy(which, o):
         return remote(
             dot_b_local.at[which],
-            dot_b.at[which, pair],
+            dot_b.at[which, plane_rank],
             sdb.at[which, o],
-            qdb.at[which, pair],
-            device(16 * ((pair + o) % 8) + member),
+            qdb.at[which, plane_rank],
+            in_plane((plane_rank + o) % 16),
         )
 
     def dot_a_start(which):
-        for o in range(1, 16):
+        for o in range(1, 8):
             dot_a_copy(which, o).start()
-        dot_a[which, member] = dot_local[which]
+        dot_a[which, column_rank] = dot_local[which]
 
     def dot_b_start(which):
-        for o in range(1, 16):
-            m = (member + o) % 16
+        for o in range(1, 8):
+            m = (column_rank + o) % 8
             remote(
                 dot_local.at[which], dot_a.at[which, m], sda.at[which, 0], qda.at[which, m], device(me)
             ).wait_recv()
         total = dot_a[which, 0]
-        for m in range(1, 16):
+        for m in range(1, 8):
             total = total + dot_a[which, m]
         dot_b_local[which] = total
-        for o in range(1, 8):
+        for o in range(1, 16):
             dot_b_copy(which, o).start()
-        dot_b[which, pair] = total
+        dot_b[which, plane_rank] = total
 
     def dot_total(which):
-        for o in range(1, 8):
-            m = (pair + o) % 8
+        for o in range(1, 16):
+            m = (plane_rank + o) % 16
             remote(
                 dot_b_local.at[which], dot_b.at[which, m], sdb.at[which, 0], qdb.at[which, m], device(me)
             ).wait_recv()
         total = dot_b[which, 0]
-        for m in range(1, 8):
+        for m in range(1, 16):
             total = total + dot_b[which, m]
         return jnp.sum(total, axis=1, keepdims=True)
 
-    halo_wait(0, full)
+    halo_wait(0, CUTS)
     for h in range(2):
         part = pl.ds(rows + 8 * h, 8)
         left, c0, c1, right = halo[0, 0, part], field[0, 0, part], field[0, 1, part], halo[0, 1, part]
@@ -443,6 +458,8 @@
 
     def gradients(i):
         for b in range(rows // 8):
+            if 8 * b % per == 0:
+                halo_wait(i, 8 * b // per)
             part = pl.ds(8 * b, 8)
             left, u0, u1, right = halo[i, 0, part], field[i, 0, part], field[i, 1, part], halo[i, 1, part]
             up0 = jnp.where(lane8 < LANES - 1, pltpu.roll(u0, LANES - 1, 1), 0.0)
@@ -480,6 +497,8 @@
             for c in range(2):
                 down = jnp.where(lane8 > 0, pltpu.roll(kind[3 + c], 1, 1), kind[5 + c])
                 after(c, part, kind[c] - kind[c + 1] + down - kind[3 + c])
+            if i < 2 and 8 * (b + 1) % per == 0:
+                halo_start(i + 1, 8 * b // per)
 
     gradients(0)
     mixing()
@@ -492,12 +511,10 @@
         field[1, c, part, :] = forced[c, part, :] - value
 
     divergence(0, first)
-    halo_start(1, rows)
     prepare_back(0)
-    halo_wait(1, rows)
+
+    gradients(1)
     send_back(0)
-
-    gradients(1)
     mixing()
     sums = [zero8, zero8]
 
@@ -508,15 +525,13 @@
         sums[1] = sums[1] + r * value
 
     divergence(1, second)
-    halo_start(2, rows)
     dots(0, sums)
     dot_a_start(0)
     prepare_back(1)
-    halo_wait(2, rows)
     dot_b_start(0)
+
+    gradients(2)
     send_back(1)
-
-    gradients(2)
     mixing()
     rr, rw = total_of(dot_total(0))[0:2]
     alpha = rr / rw
@@ -554,17 +569,19 @@
         ro_ref[pl.ds(c, slots, stride=cols), :] = r1 - step * (w - alpha * v + beta * w)
 
     sent(code_copy)
+    sent(x_copy)
     sent(f_copy)
     coef_copy.wait_send()
     for i in range(3):
-        halo_sent(i, rows if i else full)
+        for k in range(CUTS if i else CUTS + 1):
+            halo_sent(i, k)
         for g in range(8):
             here = jnp.logical_and(own_source, chaos == g)
             pl.when(jnp.logical_not(here))(lambda: back_copy(i, g).wait_send())
     for which in range(2):
+        for o in range(1, 8):
+            dot_a_copy(which, o).wait_send()
         for o in range(1, 16):
-            dot_a_copy(which, o).wait_send()
-        for o in range(1, 8):
             dot_b_copy(which, o).wait_send()
 
 
@@ -578,7 +595,7 @@
     codes = np.full((8, wide), -2.0, np.float32)
     codes[:, : len(terms)] = [code_of(t) for t in terms]
     cfg = dict(slots=slots, cols=cols, terms=terms, modes=modes, rows=rows, full=full)
-    flat = jax.ShapeDtypeStruct((slots * cols, lanes), F32)
+    flat = pltpu.VMEM((slots * cols, lanes), F32)
     vmem = pl.BlockSpec(memory_space=pltpu.VMEM)
     hbm = pl.BlockSpec(memory_space=pltpu.HBM)
     dma, V = pltpu.SemaphoreType.DMA, pltpu.VMEM
@@ -608,25 +625,25 @@
         V((3, 8, 2, PAD, lanes), F32),
         V((3, cols, PAD, lanes), F32),
         V((2, 8, lanes), F32),
+        V((2, 8, 8, lanes), F32),
+        V((2, 8, lanes), F32),
         V((2, 16, 8, lanes), F32),
-        V((2, 8, lanes), F32),
-        V((2, 8, 8, lanes), F32),
         dma((8,)),
         dma((8,)),
         dma((8,)),
         dma,
-        dma((3, 2)),
+        dma((3, CUTS + 1, 2)),
         dma((3, 8)),
+        dma((2, 8)),
         dma((2, 16)),
-        dma((2, 8)),
         dma((8,)),
         dma((8,)),
         dma((8,)),
         dma,
-        dma((3, 2)),
+        dma((3, CUTS + 1, 2)),
         dma((3, 8)),
+        dma((2, 8)),
         dma((2, 16)),
-        dma((2, 8)),
     ]
     x, r = pl.pallas_call(
         functools.partial(kernel, cfg),
@@ -635,7 +652,7 @@
         out_specs=(vmem, vmem),
         scratch_shapes=scratch,
         compiler_params=pltpu.CompilerParams(
-            collective_id=0, has_side_effects=True, vmem_limit_bytes=64 * 2**20
+            collective_id=0, has_side_effects=True, vmem_limit_bytes=60 * 2**20
         ),
     )(
         forcing.reshape(slots * cols, lanes),

time: 54.2 us -> 49.8 us (0.919)
  Pallas kernels: 50.8 us -> 47.2 us
  local copies, waits for them, and re-layouts: 2.46 us -> 1.43 us
    pallas_call x1, Pallas kernels: 50.8 us -> 47.2 us  [per_device(): pl.pallas_call(functools.partial(kernel, cfg), out_shape=(flat, flat), in...]
    unnamed x4 -> x2, local copies, waits for them, and re-layouts: 2.46 us -> 1.43 us
where the time goes in v3:
time: 49.8 us; the launch traced here: 49.3 us
  Pallas kernels  47.2 us (95%)
  local copies, waits for them, and re-layouts  1.43 us (3%)
  between operations  0.64 us (1%)
    pallas_call x1, Pallas kernels, per_device(): pl.pallas_call(functools.partial(kernel, cfg), out_shape=(flat, flat), in...  47.2 us
    unnamed x2, local copies, waits for them, and re-layouts  1.43 us

profile of v3, /device:TPU:0, one launch (start us, length us, event | category | flops | bytes accessed | tf_op | source)
XLA Modules:
  0.0 49.3 jit_solution(16899367853128197828)
XLA Ops:
  0.6 47.2 %shard_map.77 = (f32[576,128]{1,0:T(8,128)S(1)}, f32[576,128]{1,0:T(8,128)S(1)}) custom-call(f32[576,128]{1,0:T(8,128)} %bitcast.7, f32[576,128]{1,0:T(8,128)} %bitcast.8, f32[16,128]{1,0:T(8,128)} %mean_hbm.1, f32[10,16,128]{2,1,0:T(8,128)} %modes_hbm.1, s32[10,36]{1,0:T(8,128)} %bitcast.9, f32[8,288]{1,0:T(8,128)} %constant.2.clone.code_hbm), custom_call_target="tpu_custom_call" | custom-call | tf_op jit(solution)/shard_map/pallas_call | solution.py:648
  47.8 0.7 %copy.10 = f32[36,16,128]{2,1,0:T(8,128)} copy(f32[36,16,128]{2,1,0:T(8,128)S(1)} %bitcast.6) | data formatting | bytes 589824
  48.6 0.7 %copy.11 = f32[36,16,128]{2,1,0:T(8,128)} copy(f32[36,16,128]{2,1,0:T(8,128)S(1)} %bitcast.5) | data formatting | bytes 589824

commit v4 on v3

--- a/solution.py
+++ b/solution.py
@@ -14,7 +14,6 @@
 DEGREE = 3
 LANES = 128
 PAD = 40
-CUTS = 4
 
 
 def term_list(modes, degree):
@@ -190,7 +189,7 @@
 
     def piece(send, land, ssem, rsem, i):
         where = device(8 * space + i)
-        return remote(send, land, ssem.at[i], rsem.at[chaos], where)
+        return remote(send, land, ssem, rsem, where)
 
     def far_first(o):
         target_x = (xx + (2, 2, 1, 1, 3, 3, 0, 0)[o]) % 4
@@ -205,17 +204,30 @@
             pl.when(target != me)(lambda: copy_of(i).start())
             pl.when(target == me)(lambda: keep(i))
 
-    def sent(copy_of):
-        for i in range(8):
-            target = 8 * space + i
-            pl.when(target != me)(lambda: copy_of(i).wait_send())
-
     own_source = (me // 8) == space
 
-    def arrive(copy_of):
-        for g in range(8):
-            here = jnp.logical_and(own_source, chaos == g)
-            pl.when(jnp.logical_not(here))(lambda: copy_of(g).wait_recv())
+    def whole(view, ssem, rsem):
+        return remote(view, view, ssem, rsem, device(me))
+
+    def arrive(view_of, ssem, rsem):
+        pl.when(own_source)(lambda: whole(view_of(7), ssem, rsem).wait_recv())
+        pl.when(jnp.logical_not(own_source))(lambda: whole(view_of(8), ssem, rsem).wait_recv())
+
+    def sent(view_of, ssem, rsem):
+        pl.when(own_source)(lambda: whole(view_of(7), ssem, rsem).wait_send())
+        pl.when(jnp.logical_not(own_source))(lambda: whole(view_of(8), ssem, rsem).wait_send())
+
+    def codes_of(n):
+        return rcode.at[pl.ds(0, n)]
+
+    def x_of(n):
+        return rx.at[pl.ds(0, n), :, pl.ds(0, slots)]
+
+    def f_of(n):
+        return rf.at[pl.ds(0, n), :, pl.ds(0, slots)]
+
+    def back_of(n):
+        return back.at[:, pl.ds(0, 2 * n), pl.ds(0, slots)]
 
     def code_copy(i):
         return piece(scode, rcode.at[chaos], sc, qc, i)
@@ -255,20 +267,7 @@
     loads[5].wait()
     scatter(f_copy, keep(rf, sbf), packed(f_ref, sbf))
 
-    def code_wait(g):
-        return remote(scode, rcode.at[g], sc.at[0], qc.at[g], device(me))
-
-    def x_wait(g):
-        return remote(
-            sbx.at[0:2, pl.ds(0, slots)], rx.at[g, :, pl.ds(0, slots)], sx.at[0], qx.at[g], device(me)
-        )
-
-    def f_wait(g):
-        return remote(
-            sbf.at[0:2, pl.ds(0, slots)], rf.at[g, :, pl.ds(0, slots)], sf.at[0], qf.at[g], device(me)
-        )
-
-    arrive(code_wait)
+    arrive(codes_of, sc, qc)
     loads[4].wait()
     sub40 = lax.broadcasted_iota(jnp.int32, (PAD, LANES), 0)
     lane40 = lax.broadcasted_iota(jnp.int32, (PAD, LANES), 1)
@@ -301,46 +300,42 @@
             + result[:, base + 2 * LANES : base + 3 * LANES]
         )
 
-    per = rows // CUTS
-
-    def cut(k):
-        return pl.ds(per * k, per) if k < CUTS else pl.ds(rows, full - rows)
-
-    def halo_left(i, k):
+    def span(i):
+        return pl.ds(0, rows if i else full)
+
+    def halo_left(i):
         return remote(
-            field.at[i, 0, cut(k)], halo.at[i, 1, cut(k)], sh.at[i, k, 0], qh.at[i, k, 1], device(me - 1)
-        )
-
-    def halo_right(i, k):
+            field.at[i, 0, span(i)], halo.at[i, 1, span(i)], sh.at[i, 0], qh.at[i, 1], device(me - 1)
+        )
+
+    def halo_right(i):
         return remote(
-            field.at[i, 1, cut(k)], halo.at[i, 0, cut(k)], sh.at[i, k, 1], qh.at[i, k, 0], device(me + 1)
-        )
-
-    def halo_start(i, k):
-        pl.when(me > 0)(lambda: halo_left(i, k).start())
-        pl.when(me < last)(lambda: halo_right(i, k).start())
-
-    def halo_wait(i, k):
-        pl.when(me > 0)(lambda: halo_right(i, k).wait_recv())
-        pl.when(me < last)(lambda: halo_left(i, k).wait_recv())
-
-    def halo_sent(i, k):
-        pl.when(me > 0)(lambda: halo_left(i, k).wait_send())
-        pl.when(me < last)(lambda: halo_right(i, k).wait_send())
+            field.at[i, 1, span(i)], halo.at[i, 0, span(i)], sh.at[i, 1], qh.at[i, 0], device(me + 1)
+        )
+
+    def halo_start(i):
+        pl.when(me > 0)(lambda: halo_left(i).start())
+        pl.when(me < last)(lambda: halo_right(i).start())
+
+    def halo_wait(i):
+        pl.when(me > 0)(lambda: halo_right(i).wait_recv())
+        pl.when(me < last)(lambda: halo_left(i).wait_recv())
+
+    def halo_sent(i):
+        pl.when(me > 0)(lambda: halo_left(i).wait_send())
+        pl.when(me < last)(lambda: halo_right(i).wait_send())
 
     coef_copy.wait_recv()
     local = core == zz
     for c in range(2):
         field[0, c, rows:full, :] = jnp.where(local, scoef[0, c], rcoef[c])
-    halo_start(0, CUTS)
-
-    arrive(x_wait)
+
+    arrive(x_of, sx, qx)
     got = select(rx[:, 0].reshape(8 * PAD, LANES), rx[:, 1].reshape(8 * PAD, LANES), True)
     for c in range(2):
         field[0, c, 0:rows, :] = column(got, c)[0:rows]
 
-    for k in range(CUTS):
-        halo_start(0, k)
+    halo_start(0)
 
     lane8 = lax.broadcasted_iota(jnp.int32, (8, LANES), 1)
 
@@ -348,18 +343,9 @@
         return remote(
             outs.at[i, g, :, pl.ds(0, slots)],
             back.at[i, pl.ds(2 * (me % 8), 2), pl.ds(0, slots)],
-            so.at[i, g],
-            qo.at[i, me % 8],
+            so,
+            qo,
             (me // 8, g),
-        )
-
-    def back_wait(i, j):
-        return remote(
-            outs.at[i, 0, :, pl.ds(0, slots)],
-            back.at[i, pl.ds(2 * j, 2), pl.ds(0, slots)],
-            so.at[i, 0],
-            qo.at[i, j],
-            (space, chaos),
         )
 
     def prepare_back(i):
@@ -388,8 +374,8 @@
         return remote(
             dot_local.at[which],
             dot_a.at[which, column_rank],
-            sda.at[which, o],
-            qda.at[which, column_rank],
+            sda,
+            qda.at[which],
             in_column((column_rank + o) % 8),
         )
 
@@ -397,8 +383,8 @@
         return remote(
             dot_b_local.at[which],
             dot_b.at[which, plane_rank],
-            sdb.at[which, o],
-            qdb.at[which, plane_rank],
+            sdb,
+            qdb.at[which],
             in_plane((plane_rank + o) % 16),
         )
 
@@ -408,11 +394,7 @@
         dot_a[which, column_rank] = dot_local[which]
 
     def dot_b_start(which):
-        for o in range(1, 8):
-            m = (column_rank + o) % 8
-            remote(
-                dot_local.at[which], dot_a.at[which, m], sda.at[which, 0], qda.at[which, m], device(me)
-            ).wait_recv()
+        whole(dot_a.at[which, pl.ds(0, 7)], sda, qda.at[which]).wait_recv()
         total = dot_a[which, 0]
         for m in range(1, 8):
             total = total + dot_a[which, m]
@@ -422,17 +404,13 @@
         dot_b[which, plane_rank] = total
 
     def dot_total(which):
-        for o in range(1, 16):
-            m = (plane_rank + o) % 16
-            remote(
-                dot_b_local.at[which], dot_b.at[which, m], sdb.at[which, 0], qdb.at[which, m], device(me)
-            ).wait_recv()
+        whole(dot_b.at[which, pl.ds(0, 15)], sdb, qdb.at[which]).wait_recv()
         total = dot_b[which, 0]
         for m in range(1, 16):
             total = total + dot_b[which, m]
         return jnp.sum(total, axis=1, keepdims=True)
 
-    halo_wait(0, CUTS)
+    halo_wait(0)
     for h in range(2):
         part = pl.ds(rows + 8 * h, 8)
         left, c0, c1, right = halo[0, 0, part], field[0, 0, part], field[0, 1, part], halo[0, 1, part]
@@ -457,9 +435,9 @@
         return [sums[n : n + 1] for n in range(3)]
 
     def gradients(i):
+        if i:
+            halo_wait(i)
         for b in range(rows // 8):
-            if 8 * b % per == 0:
-                halo_wait(i, 8 * b // per)
             part = pl.ds(8 * b, 8)
             left, u0, u1, right = halo[i, 0, part], field[i, 0, part], field[i, 1, part], halo[i, 1, part]
             up0 = jnp.where(lane8 < LANES - 1, pltpu.roll(u0, LANES - 1, 1), 0.0)
@@ -497,12 +475,10 @@
             for c in range(2):
                 down = jnp.where(lane8 > 0, pltpu.roll(kind[3 + c], 1, 1), kind[5 + c])
                 after(c, part, kind[c] - kind[c + 1] + down - kind[3 + c])
-            if i < 2 and 8 * (b + 1) % per == 0:
-                halo_start(i + 1, 8 * b // per)
 
     gradients(0)
     mixing()
-    arrive(f_wait)
+    arrive(f_of, sf, qf)
     got = select(rf[:, 0].reshape(8 * PAD, LANES), rf[:, 1].reshape(8 * PAD, LANES), True)
     for c in range(2):
         forced[c] = column(got, c)[0:rows]
@@ -511,6 +487,7 @@
         field[1, c, part, :] = forced[c, part, :] - value
 
     divergence(0, first)
+    halo_start(1)
     prepare_back(0)
 
     gradients(1)
@@ -525,6 +502,7 @@
         sums[1] = sums[1] + r * value
 
     divergence(1, second)
+    halo_start(2)
     dots(0, sums)
     dot_a_start(0)
     prepare_back(1)
@@ -556,10 +534,7 @@
     beta = rr1 / rr
     step = rr1 / (rar + beta * cross + beta * beta * rw)
 
-    for j in range(8):
-        here = jnp.logical_and(own_source, me % 8 == j)
-        for i in range(3):
-            pl.when(jnp.logical_not(here))(lambda: back_wait(i, j).wait_recv())
+    arrive(back_of, so, qo)
 
     for c in range(cols):
         r0, w, v = back[0, c, 0:slots], back[1, c, 0:slots], back[2, c, 0:slots]
@@ -568,21 +543,15 @@
         r1 = r0 - alpha * w
         ro_ref[pl.ds(c, slots, stride=cols), :] = r1 - step * (w - alpha * v + beta * w)
 
-    sent(code_copy)
-    sent(x_copy)
-    sent(f_copy)
+    sent(codes_of, sc, qc)
+    sent(x_of, sx, qx)
+    sent(f_of, sf, qf)
+    sent(back_of, so, qo)
     coef_copy.wait_send()
     for i in range(3):
-        for k in range(CUTS if i else CUTS + 1):
-            halo_sent(i, k)
-        for g in range(8):
-            here = jnp.logical_and(own_source, chaos == g)
-            pl.when(jnp.logical_not(here))(lambda: back_copy(i, g).wait_send())
-    for which in range(2):
-        for o in range(1, 8):
-            dot_a_copy(which, o).wait_send()
-        for o in range(1, 16):
-            dot_b_copy(which, o).wait_send()
+        halo_sent(i)
+    whole(dot_a.at[:, pl.ds(0, 7)], sda, qda.at[0]).wait_send()
+    whole(dot_b.at[:, pl.ds(0, 15)], sdb, qdb.at[0]).wait_send()
 
 
 def per_device(forcing, start_guess, mean_field, mode_fields, multi_index, coupled_slot):
@@ -628,22 +597,22 @@
         V((2, 8, 8, lanes), F32),
         V((2, 8, lanes), F32),
         V((2, 16, 8, lanes), F32),
-        dma((8,)),
-        dma((8,)),
-        dma((8,)),
-        dma,
-        dma((3, CUTS + 1, 2)),
-        dma((3, 8)),
-        dma((2, 8)),
-        dma((2, 16)),
-        dma((8,)),
-        dma((8,)),
-        dma((8,)),
-        dma,
-        dma((3, CUTS + 1, 2)),
-        dma((3, 8)),
-        dma((2, 8)),
-        dma((2, 16)),
+        dma,
+        dma,
+        dma,
+        dma,
+        dma((3, 2)),
+        dma,
+        dma,
+        dma,
+        dma,
+        dma,
+        dma,
+        dma,
+        dma((3, 2)),
+        dma,
+        dma((2,)),
+        dma((2,)),
     ]
     x, r = pl.pallas_call(
         functools.partial(kernel, cfg),

time: 49.8 us -> 48 us (0.964)
  Pallas kernels: 47.2 us -> 45.7 us
    pallas_call x1, Pallas kernels: 47.2 us -> 45.7 us  [per_device(): pl.pallas_call(functools.partial(kernel, cfg), out_shape=(flat, flat), in...]
where the time goes in v4:
time: 48 us; the launch traced here: 47.7 us
  Pallas kernels  45.7 us (95%)
  local copies, waits for them, and re-layouts  1.43 us (3%)
  between operations  0.64 us (1%)
    pallas_call x1, Pallas kernels, per_device(): pl.pallas_call(functools.partial(kernel, cfg), out_shape=(flat, flat), in...  45.7 us
    unnamed x2, local copies, waits for them, and re-layouts  1.43 us

profile of v4, /device:TPU:0, one launch (start us, length us, event | category | flops | bytes accessed | tf_op | source)
XLA Modules:
  0.0 47.7 jit_solution(4734982188481059419)
XLA Ops:
  0.6 45.7 %shard_map.77 = (f32[576,128]{1,0:T(8,128)S(1)}, f32[576,128]{1,0:T(8,128)S(1)}) custom-call(f32[576,128]{1,0:T(8,128)} %bitcast.7, f32[576,128]{1,0:T(8,128)} %bitcast.8, f32[16,128]{1,0:T(8,128)} %mean_hbm.1, f32[10,16,128]{2,1,0:T(8,128)} %modes_hbm.1, s32[10,36]{1,0:T(8,128)} %bitcast.9, f32[8,288]{1,0:T(8,128)} %constant.2.clone.code_hbm), custom_call_target="tpu_custom_call" | custom-call | tf_op jit(solution)/shard_map/pallas_call | solution.py:617
  46.3 0.7 %copy.10 = f32[36,16,128]{2,1,0:T(8,128)} copy(f32[36,16,128]{2,1,0:T(8,128)S(1)} %bitcast.6) | data formatting | bytes 589824
  47.0 0.7 %copy.11 = f32[36,16,128]{2,1,0:T(8,128)} copy(f32[36,16,128]{2,1,0:T(8,128)S(1)} %bitcast.5) | data formatting | bytes 589824

commit v5 on v4

--- a/solution.py
+++ b/solution.py
@@ -172,6 +172,86 @@
     scode[...] = jnp.full((8, LANES), -1.0, F32)
     scode[:, 0:slots] = jnp.broadcast_to(code, (8, slots))
 
+    loads[1].wait()
+    greeted = 15 + 7 + 9 + jnp.where(me > 0, 1, 0) + jnp.where(me < last, 1, 0)
+    pl.semaphore_wait(barrier, greeted)
+
+    def piece(send, land, ssem, rsem, i):
+        where = device(8 * space + i)
+        return remote(send, land, ssem, rsem, where)
+
+    def far_first(o):
+        target_x = (xx + (2, 2, 1, 1, 3, 3, 0, 0)[o]) % 4
+        return 2 * (target_x + core * (3 - 2 * target_x)) + o % 2
+
+    def scatter(copy_of, keep, ready=None):
+        for o in range(8):
+            i = far_first(o)
+            target = 8 * space + i
+            if ready is not None:
+                ready(i)
+            pl.when(target != me)(lambda: copy_of(i).start())
+            pl.when(target == me)(lambda: keep(i))
+
+    own_source = (me // 8) == space
+
+    def whole(view, ssem, rsem):
+        return remote(view, view, ssem, rsem, device(me))
+
+    def arrive(view_of, ssem, rsem):
+        pl.when(own_source)(lambda: whole(view_of(7), ssem, rsem).wait_recv())
+        pl.when(jnp.logical_not(own_source))(lambda: whole(view_of(8), ssem, rsem).wait_recv())
+
+    def sent(view_of, ssem, rsem):
+        pl.when(own_source)(lambda: whole(view_of(7), ssem, rsem).wait_send())
+        pl.when(jnp.logical_not(own_source))(lambda: whole(view_of(8), ssem, rsem).wait_send())
+
+    def codes_of(n):
+        return rcode.at[pl.ds(0, n)]
+
+    def x_of(n):
+        return rx.at[pl.ds(0, n), :, pl.ds(0, slots)]
+
+    def f_of(n):
+        return rf.at[pl.ds(0, n), :, pl.ds(0, slots)]
+
+    def back_of(n):
+        return back.at[:, pl.ds(0, 2 * n), pl.ds(0, slots)]
+
+    def code_copy(i):
+        return piece(scode, rcode.at[chaos], sc, qc, i)
+
+    def x_copy(i):
+        return piece(
+            sbx.at[pl.ds(2 * i, 2), pl.ds(0, slots)], rx.at[chaos, :, pl.ds(0, slots)], sx, qx, i
+        )
+
+    def f_copy(i):
+        return piece(
+            sbf.at[pl.ds(2 * i, 2), pl.ds(0, slots)], rf.at[chaos, :, pl.ds(0, slots)], sf, qf, i
+        )
+
+    def keep_code(i):
+        rcode[chaos] = scode[...]
+
+    def keep(land, send):
+        def run(i):
+            for c in range(2):
+                land[chaos, c, 0:slots, :] = send[2 * i + c, 0:slots, :]
+
+        return run
+
+    def packed(src, dst):
+        def run(i):
+            for c in range(2):
+                dst[2 * i + c, 0:slots, :] = src[pl.ds(2 * i + c, slots, stride=cols), :]
+
+        return run
+
+    sibling = me + 1 - 2 * core
+    coef_copy = remote(scoef.at[1], rcoef, sk, qk, device(sibling))
+    scatter(code_copy, keep_code)
+    scatter(x_copy, keep(rx, sbx), packed(x_ref, sbx))
     loads[2].wait()
     loads[3].wait()
     mine = 2 * lane_at + core
@@ -182,88 +262,8 @@
             scoef[which, c, 0:1, :] = mean_ref[pl.ds(first + c, 1), :]
             for k in range(modes):
                 scoef[which, c, 1 + k : 2 + k, :] = modes_ref[k, pl.ds(first + c, 1), :]
-
-    loads[1].wait()
-    greeted = 15 + 7 + 9 + jnp.where(me > 0, 1, 0) + jnp.where(me < last, 1, 0)
-    pl.semaphore_wait(barrier, greeted)
-
-    def piece(send, land, ssem, rsem, i):
-        where = device(8 * space + i)
-        return remote(send, land, ssem, rsem, where)
-
-    def far_first(o):
-        target_x = (xx + (2, 2, 1, 1, 3, 3, 0, 0)[o]) % 4
-        return 2 * (target_x + core * (3 - 2 * target_x)) + o % 2
-
-    def scatter(copy_of, keep, ready=None):
-        for o in range(8):
-            i = far_first(o)
-            target = 8 * space + i
-            if ready is not None:
-                ready(i)
-            pl.when(target != me)(lambda: copy_of(i).start())
-            pl.when(target == me)(lambda: keep(i))
-
-    own_source = (me // 8) == space
-
-    def whole(view, ssem, rsem):
-        return remote(view, view, ssem, rsem, device(me))
-
-    def arrive(view_of, ssem, rsem):
-        pl.when(own_source)(lambda: whole(view_of(7), ssem, rsem).wait_recv())
-        pl.when(jnp.logical_not(own_source))(lambda: whole(view_of(8), ssem, rsem).wait_recv())
-
-    def sent(view_of, ssem, rsem):
-        pl.when(own_source)(lambda: whole(view_of(7), ssem, rsem).wait_send())
-        pl.when(jnp.logical_not(own_source))(lambda: whole(view_of(8), ssem, rsem).wait_send())
-
-    def codes_of(n):
-        return rcode.at[pl.ds(0, n)]
-
-    def x_of(n):
-        return rx.at[pl.ds(0, n), :, pl.ds(0, slots)]
-
-    def f_of(n):
-        return rf.at[pl.ds(0, n), :, pl.ds(0, slots)]
-
-    def back_of(n):
-        return back.at[:, pl.ds(0, 2 * n), pl.ds(0, slots)]
-
-    def code_copy(i):
-        return piece(scode, rcode.at[chaos], sc, qc, i)
-
-    def x_copy(i):
-        return piece(
-            sbx.at[pl.ds(2 * i, 2), pl.ds(0, slots)], rx.at[chaos, :, pl.ds(0, slots)], sx, qx, i
-        )
-
-    def f_copy(i):
-        return piece(
-            sbf.at[pl.ds(2 * i, 2), pl.ds(0, slots)], rf.at[chaos, :, pl.ds(0, slots)], sf, qf, i
-        )
-
-    def keep_code(i):
-        rcode[chaos] = scode[...]
-
-    def keep(land, send):
-        def run(i):
-            for c in range(2):
-                land[chaos, c, 0:slots, :] = send[2 * i + c, 0:slots, :]
-
-        return run
-
-    def packed(src, dst):
-        def run(i):
-            for c in range(2):
-                dst[2 * i + c, 0:slots, :] = src[pl.ds(2 * i + c, slots, stride=cols), :]
-
-        return run
-
-    sibling = me + 1 - 2 * core
-    coef_copy = remote(scoef.at[1], rcoef, sk, qk, device(sibling))
-    scatter(code_copy, keep_code)
     coef_copy.start()
-    scatter(x_copy, keep(rx, sbx), packed(x_ref, sbx))
+
     loads[5].wait()
     scatter(f_copy, keep(rf, sbf), packed(f_ref, sbf))
 
@@ -430,9 +430,6 @@
         ]
         for n, kind in enumerate(kinds):
             faces[pl.ds(64 * h + n, 8, stride=8), :] = kind
-
-    def total_of(sums):
-        return [sums[n : n + 1] for n in range(3)]
 
     def gradients(i):
         if i:
@@ -493,44 +490,37 @@
     gradients(1)
     send_back(0)
     mixing()
-    sums = [zero8, zero8]
 
     def second(c, part, value):
         field[2, c, part, :] = value
-        r = field[1, c, part, :]
-        sums[0] = sums[0] + r * r
-        sums[1] = sums[1] + r * value
 
     divergence(1, second)
     halo_start(2)
-    dots(0, sums)
-    dot_a_start(0)
     prepare_back(1)
-    dot_b_start(0)
 
     gradients(2)
     send_back(1)
     mixing()
-    rr, rw = total_of(dot_total(0))[0:2]
-    alpha = rr / rw
-    sums = [zero8, zero8, zero8]
+    sums = [zero8] * 5
 
     def third(c, part, value):
         field[3, c, part, :] = value
         r, w = field[1, c, part, :], field[2, c, part, :]
-        r1 = r - alpha * w
-        ar1 = w - alpha * value
-        sums[0] = sums[0] + r1 * r1
-        sums[1] = sums[1] + r1 * ar1
-        sums[2] = sums[2] + (r1 * w + r * ar1)
+        for n, (a, b) in enumerate(((r, r), (r, w), (w, w), (r, value), (w, value))):
+            sums[n] = sums[n] + a * b
 
     divergence(2, third)
-    dots(1, sums)
-    dot_a_start(1)
+    dots(0, sums)
+    dot_a_start(0)
     prepare_back(2)
     send_back(2)
-    dot_b_start(1)
-    rr1, rar, cross = total_of(dot_total(1))
+    dot_b_start(0)
+    total = dot_total(0)
+    rr, rw, ww, rv, wv = (total[n : n + 1] for n in range(5))
+    alpha = rr / rw
+    rr1 = rr - 2.0 * alpha * rw + alpha * alpha * ww
+    rar = rw - alpha * (rv + ww) + alpha * alpha * wv
+    cross = 2.0 * rw - alpha * (ww + rv)
     beta = rr1 / rr
     step = rr1 / (rar + beta * cross + beta * beta * rw)
 
@@ -550,8 +540,8 @@
     coef_copy.wait_send()
     for i in range(3):
         halo_sent(i)
-    whole(dot_a.at[:, pl.ds(0, 7)], sda, qda.at[0]).wait_send()
-    whole(dot_b.at[:, pl.ds(0, 15)], sdb, qdb.at[0]).wait_send()
+    whole(dot_a.at[0, pl.ds(0, 7)], sda, qda.at[0]).wait_send()
+    whole(dot_b.at[0, pl.ds(0, 15)], sdb, qdb.at[0]).wait_send()
 
 
 def per_device(forcing, start_guess, mean_field, mode_fields, multi_index, coupled_slot):
@@ -593,10 +583,10 @@
         V((128, lanes), F32),
         V((3, 8, 2, PAD, lanes), F32),
         V((3, cols, PAD, lanes), F32),
-        V((2, 8, lanes), F32),
-        V((2, 8, 8, lanes), F32),
-        V((2, 8, lanes), F32),
-        V((2, 16, 8, lanes), F32),
+        V((1, 8, lanes), F32),
+        V((1, 8, 8, lanes), F32),
+        V((1, 8, lanes), F32),
+        V((1, 16, 8, lanes), F32),
         dma,
         dma,
         dma,
@@ -611,8 +601,8 @@
         dma,
         dma((3, 2)),
         dma,
-        dma((2,)),
-        dma((2,)),
+        dma((1,)),
+        dma((1,)),
     ]
     x, r = pl.pallas_call(
         functools.partial(kernel, cfg),

time: 48 us -> 45.7 us (0.952)
  Pallas kernels: 45.7 us -> 43.1 us
    pallas_call x1, Pallas kernels: 45.7 us -> 43.1 us  [per_device(): pl.pallas_call(functools.partial(kernel, cfg), out_shape=(flat, flat), in...]
where the time goes in v5:
time: 45.7 us; the launch traced here: 45.1 us
  Pallas kernels  43.1 us (94%)
  local copies, waits for them, and re-layouts  1.43 us (3%)
  between operations  0.64 us (1%)
    pallas_call x1, Pallas kernels, per_device(): pl.pallas_call(functools.partial(kernel, cfg), out_shape=(flat, flat), in...  43.1 us
    unnamed x2, local copies, waits for them, and re-layouts  1.43 us

profile of v5, /device:TPU:0, one launch (start us, length us, event | category | flops | bytes accessed | tf_op | source)
XLA Modules:
  0.0 45.1 jit_solution(7742589636595693833)
XLA Ops:
  0.6 43.1 %shard_map.77 = (f32[576,128]{1,0:T(8,128)S(1)}, f32[576,128]{1,0:T(8,128)S(1)}) custom-call(f32[576,128]{1,0:T(8,128)} %bitcast.7, f32[576,128]{1,0:T(8,128)} %bitcast.8, f32[16,128]{1,0:T(8,128)} %mean_hbm.1, f32[10,16,128]{2,1,0:T(8,128)} %modes_hbm.1, s32[10,36]{1,0:T(8,128)} %bitcast.9, f32[8,288]{1,0:T(8,128)} %constant.2.clone.code_hbm), custom_call_target="tpu_custom_call" | custom-call | tf_op jit(solution)/shard_map/pallas_call | solution.py:607
  43.7 0.7 %copy.10 = f32[36,16,128]{2,1,0:T(8,128)} copy(f32[36,16,128]{2,1,0:T(8,128)S(1)} %bitcast.6) | data formatting | bytes 589824
  44.4 0.7 %copy.11 = f32[36,16,128]{2,1,0:T(8,128)} copy(f32[36,16,128]{2,1,0:T(8,128)S(1)} %bitcast.5) | data formatting | bytes 589824

commit v6 on v5

--- a/solution.py
+++ b/solution.py
@@ -513,8 +513,8 @@
     dots(0, sums)
     dot_a_start(0)
     prepare_back(2)
+    dot_b_start(0)
     send_back(2)
-    dot_b_start(0)
     total = dot_total(0)
     rr, rw, ww, rv, wv = (total[n : n + 1] for n in range(5))
     alpha = rr / rw

time: 45.7 us -> 47.1 us (1.031); the launches traced: 45.1 us -> 47 us
  Pallas kernels: 43.1 us -> 44.9 us
    pallas_call x1, Pallas kernels: 43.1 us -> 44.9 us  [per_device(): pl.pallas_call(functools.partial(kernel, cfg), out_shape=(flat, flat), in...]
where the time goes in v6:
time: 47.1 us; the launch traced here: 47 us
  Pallas kernels  44.9 us (95%)
  local copies, waits for them, and re-layouts  1.43 us (3%)
  between operations  0.64 us (1%)
    pallas_call x1, Pallas kernels, per_device(): pl.pallas_call(functools.partial(kernel, cfg), out_shape=(flat, flat), in...  44.9 us
    unnamed x2, local copies, waits for them, and re-layouts  1.43 us

profile of v6, /device:TPU:0, one launch (start us, length us, event | category | flops | bytes accessed | tf_op | source)
XLA Modules:
  0.0 47.0 jit_solution(18201623929434745119)
XLA Ops:
  0.6 44.9 %shard_map.77 = (f32[576,128]{1,0:T(8,128)S(1)}, f32[576,128]{1,0:T(8,128)S(1)}) custom-call(f32[576,128]{1,0:T(8,128)} %bitcast.7, f32[576,128]{1,0:T(8,128)} %bitcast.8, f32[16,128]{1,0:T(8,128)} %mean_hbm.1, f32[10,16,128]{2,1,0:T(8,128)} %modes_hbm.1, s32[10,36]{1,0:T(8,128)} %bitcast.9, f32[8,288]{1,0:T(8,128)} %constant.2.clone.code_hbm), custom_call_target="tpu_custom_call" | custom-call | tf_op jit(solution)/shard_map/pallas_call | solution.py:607
  45.6 0.7 %copy.10 = f32[36,16,128]{2,1,0:T(8,128)} copy(f32[36,16,128]{2,1,0:T(8,128)S(1)} %bitcast.6) | data formatting | bytes 589824
  46.3 0.7 %copy.11 = f32[36,16,128]{2,1,0:T(8,128)} copy(f32[36,16,128]{2,1,0:T(8,128)S(1)} %bitcast.5) | data formatting | bytes 589824

commit v7 on v5

--- a/solution.py
+++ b/solution.py
@@ -498,8 +498,8 @@
     halo_start(2)
     prepare_back(1)
 
+    send_back(1)
     gradients(2)
-    send_back(1)
     mixing()
     sums = [zero8] * 5
 

time: 45.7 us -> 46.8 us (1.024)
  Pallas kernels: 43.1 us -> 44.4 us
    pallas_call x1, Pallas kernels: 43.1 us -> 44.4 us  [per_device(): pl.pallas_call(functools.partial(kernel, cfg), out_shape=(flat, flat), in...]
where the time goes in v7:
time: 46.8 us; the launch traced here: 46.5 us
  Pallas kernels  44.4 us (95%)
  local copies, waits for them, and re-layouts  1.43 us (3%)
  between operations  0.64 us (1%)
    pallas_call x1, Pallas kernels, per_device(): pl.pallas_call(functools.partial(kernel, cfg), out_shape=(flat, flat), in...  44.4 us
    unnamed x2, local copies, waits for them, and re-layouts  1.43 us

profile of v7, /device:TPU:0, one launch (start us, length us, event | category | flops | bytes accessed | tf_op | source)
XLA Modules:
  0.0 46.5 jit_solution(3309750358208664499)
XLA Ops:
  0.6 44.4 %shard_map.77 = (f32[576,128]{1,0:T(8,128)S(1)}, f32[576,128]{1,0:T(8,128)S(1)}) custom-call(f32[576,128]{1,0:T(8,128)} %bitcast.7, f32[576,128]{1,0:T(8,128)} %bitcast.8, f32[16,128]{1,0:T(8,128)} %mean_hbm.1, f32[10,16,128]{2,1,0:T(8,128)} %modes_hbm.1, s32[10,36]{1,0:T(8,128)} %bitcast.9, f32[8,288]{1,0:T(8,128)} %constant.2.clone.code_hbm), custom_call_target="tpu_custom_call" | custom-call | tf_op jit(solution)/shard_map/pallas_call | solution.py:607
  45.0 0.7 %copy.10 = f32[36,16,128]{2,1,0:T(8,128)} copy(f32[36,16,128]{2,1,0:T(8,128)S(1)} %bitcast.6) | data formatting | bytes 589824
  45.7 0.7 %copy.11 = f32[36,16,128]{2,1,0:T(8,128)} copy(f32[36,16,128]{2,1,0:T(8,128)S(1)} %bitcast.5) | data formatting | bytes 589824
